TPU v7x, 32 devices: a whole 2x2x4 slice. The times are simulated.
32 devices in a mesh: dom: 8 (over z, x), bud: 4 (over y, core).
Axes of the slice: x: 2, y: 2, z: 4, core: 2. Of those that a mesh axis runs over, the one named last changes fastest.
Arguments:
- right_side: float32 [3, 32, 64, 128], P(None, 'dom', 'bud'), may hold values from -8 to 8
- stiffness: float32 [32, 64, 128], P('dom', 'bud'), may hold values from 0.5 to 2
- coupling: float32 [27, 3, 3], replicated, may hold values from -2 to 3, as said below
- iterate_in: float32 [3, 32, 64, 128], P(None, 'dom', 'bud'), may hold values from -8 to 8
- residual_in: float32 [3, 32, 64, 128], P(None, 'dom', 'bud'), may hold values from -20 to 20
- direction_in: float32 [3, 32, 64, 128], P(None, 'dom', 'bud'), may hold values from -20 to 20
- backup_in: float32 [2, 3, 32, 64, 128], P(None, None, 'dom', 'bud'), may hold values from -8 to 8
- beta_prev: float32 [1], replicated, may hold values from 0.3 to 0.9
- fail_column: int32 [8], P('dom'), may hold values from 0 to 3, as said below
- buddy_bit: int32 [8], P('dom'), may hold values from 0 to 1
Outputs:
- iterate: float32 [3, 32, 64, 128], P(None, 'dom', 'bud')
- residual: float32 [3, 32, 64, 128], P(None, 'dom', 'bud')
- backup: float32 [2, 3, 32, 64, 128], P(None, None, 'dom', 'bud')
Inputs may be any that keep to these rules, and one draw needn't show every extreme that they name: `fail_column`: every column index appears among the lost columns. The buddy of block (i, k) is the block (i, k with binary digit buddy_bit[i] flipped). coupling[26 - o] is the transpose of coupling[o]; each diagonal entry of coupling[13] exceeds 1.02 times the sum of the magnitudes of all other entries of its row over all 27 blocks.
All inputs are finite; a program needn't handle non-finite values.
Results may differ from a plain program's by a relative error of at most 0.00015.
Values sent between devices are 32-bit elements; how exact they have to be, the bound alone decides.
A program may use at most 64 MiB of HBM per device.

v0:
```python
import functools

import jax
import jax.numpy as jnp
from jax import lax
from jax.experimental import pallas as pl
from jax.experimental.pallas import tpu as pltpu
from jax.sharding import PartitionSpec as P

SWEEPS = 4
LOW = 0.01
HIGH = 1.99
SIDES = [(sx, sy) for sx in (-1, 0, 1) for sy in (-1, 0, 1) if (sx, sy) != (0, 0)]
Y0 = 8


def kernel(
    nd, nb, levels,
    rhs_h, stiff_h, cpl_h, x_h, r_h, p_h, bk, beta, fc, bb,
    x_out, r0, bsend, b_out, img, s_out, coef,
    rhs, stiff, cpl, x_in, r_in, p_in, in_sems,
    pads, padl, flat, ysend, yrecv, csend, crecv, saved, brecv,
    inv, img3, target, solved, update,
    red, red1, red2, rrecv, brecv2,
    hs, hr, ss, sr, bs, br, d1s, d1r, d2s, d2r,
):
    nx, ny, nz = stiff.shape
    step = 2 if nx % 2 == 0 else 1
    dom, bud = lax.axis_index("dom"), lax.axis_index("bud")

    def has(side):
        sx, sy = side
        ok = None
        for cond in (
            ([dom > 0] if sx < 0 else [dom < nd - 1] if sx > 0 else [])
            + ([bud > 0] if sy < 0 else [bud < nb - 1] if sy > 0 else [])
        ):
            ok = cond if ok is None else jnp.logical_and(ok, cond)
        return ok

    def remote(src, dst, send, recv, d, b):
        return pltpu.make_async_remote_copy(
            src_ref=src, dst_ref=dst, send_sem=send, recv_sem=recv,
            device_id={"dom": d, "bud": b}, device_id_type=pl.DeviceIdType.MESH,
        )

    def flip(level):
        stride = 1 << level
        return bud + stride * (1 - 2 * (lax.rem(bud // stride, 2)))

    coef[...] = jnp.zeros(coef.shape, coef.dtype)
    loads = {}
    for i, (name, src, dst) in enumerate((
        ("cpl", cpl_h, cpl), ("stiff", stiff_h, stiff), ("x", x_h, x_in),
        ("p", p_h, p_in), ("r", r_h, r_in), ("rhs", rhs_h, rhs),
    )):
        loads[name] = pltpu.make_async_copy(src, dst, in_sems.at[i])
        loads[name].start()

    for pad in [pads.at[e] for e in range(4)] + [padl]:
        face = jnp.zeros((3, ny + 2 * Y0, nz), pad.dtype)
        pad[:, 0] = face
        pad[:, nx + 1] = face
        rim = jnp.zeros((3, nx, Y0, nz), pad.dtype)
        pad[:, 1:nx + 1, 0:Y0, :] = rim
        pad[:, 1:nx + 1, Y0 + ny:ny + 2 * Y0, :] = rim
    yrecv[...] = jnp.zeros(yrecv.shape, yrecv.dtype)
    crecv[...] = jnp.zeros(crecv.shape, crecv.dtype)

    barrier = pltpu.get_barrier_semaphore()

    def greet(d, b):
        pl.semaphore_signal(
            barrier, inc=1, device_id={"dom": d, "bud": b},
            device_id_type=pl.DeviceIdType.MESH,
        )

    for j in range(1, nb):
        greet(dom, lax.rem(bud + j, nb))
    for j in range(1, nd):
        greet(lax.rem(dom + j, nd), bud)
    diagonals = [s for s in SIDES if s[0] != 0 and s[1] != 0]
    for side in diagonals:
        @pl.when(has(side))
        def _(side=side):
            greet(dom + side[0], bud + side[1])

    for name in ("cpl", "stiff", "x"):
        loads[name].wait()
    me_failed = jnp.full((1, ny, nz), fc[0], jnp.int32) == bud
    bit_here = jnp.full((1, ny, nz), bb[0], jnp.int32)

    def halo_copies(e, which, side):
        sx, sy = side
        i = SIDES.index(side)
        o = SIDES.index((-sx, -sy))
        to = (dom + sx, bud + sy)
        if sy == 0:
            src = flat.at[e, :, nx - 1 if sx > 0 else 0]
            dst = pads.at[e, :, 0 if sx > 0 else nx + 1, pl.ds(Y0, ny), :]
        elif sx == 0:
            src = ysend.at[e, 1 if sy > 0 else 0]
            dst = yrecv.at[e, 0 if sy > 0 else 1]
        else:
            src = csend.at[e, i]
            dst = crecv.at[e, o]
        return remote(src, dst, hs.at[e, i], hr.at[e, o], *to)

    def landing(e, side):
        sx, sy = side
        i = SIDES.index(side)
        if sy == 0:
            src = flat.at[e, :, nx - 1 if sx > 0 else 0]
            dst = pads.at[e, :, nx + 1 if sx > 0 else 0, pl.ds(Y0, ny), :]
        elif sx == 0:
            src = ysend.at[e, 1 if sy > 0 else 0]
            dst = yrecv.at[e, 1 if sy > 0 else 0]
        else:
            src = csend.at[e, i]
            dst = crecv.at[e, i]
        return remote(src, dst, hs.at[e, i], hr.at[e, i], dom + sx, bud + sy)

    def pack(e, corners=None):
        for c in range(3):
            for x in range(nx if corners is not True else 0):
                row = c * nx + x
                ysend[e, 0, row:row + 1, :] = flat[e, c, x, 0:1, :]
                ysend[e, 1, row:row + 1, :] = flat[e, c, x, ny - 1:ny, :]
            for i, (sx, sy) in enumerate(SIDES):
                if sx != 0 and sy != 0 and corners is not False:
                    y = ny - 1 if sy > 0 else 0
                    csend[e, i, c:c + 1, :] = flat[e, c, nx - 1 if sx > 0 else 0, y:y + 1, :]

    def send_halo(e, sides=SIDES):
        for side in sides:
            @pl.when(has(side))
            def _(side=side):
                halo_copies(e, 0, side).start()

    def take_halo(e):
        for side in SIDES:
            @pl.when(has(side))
            def _(side=side):
                landing(e, side).wait_recv()
        for c in range(3):
            for x in range(nx):
                row = c * nx + x
                pads[e, c, x + 1, Y0 - 1:Y0, :] = yrecv[e, 0, row:row + 1, :]
                pads[e, c, x + 1, Y0 + ny:Y0 + ny + 1, :] = yrecv[e, 1, row:row + 1, :]
            for i, (sx, sy) in enumerate(SIDES):
                if sx != 0 and sy != 0:
                    y = Y0 + ny if sy > 0 else Y0 - 1
                    pads[e, c, nx + 1 if sx > 0 else 0, y:y + 1, :] = crecv[e, i, c:c + 1, :]

    def end_halo(e):
        for side in SIDES:
            @pl.when(has(side))
            def _(side=side):
                halo_copies(e, 0, side).wait_send()

    lane = lax.broadcasted_iota(jnp.int32, (step, ny, nz), 2)

    def apply(pad, out):
        @pl.loop(0, nx // step)
        def _(j):
            x = j * step
            acc = [[None] * 3 for _ in range(3)]
            for dx in range(3):
                for dy in range(3):
                    for b in range(3):
                        w = pad[b, pl.ds(x + dx, step), Y0 - 1 + dy:Y0 - 1 + dy + ny, :]
                        for dz in range(3):
                            o = (dx * 3 + dy) * 3 + dz
                            for a in range(3):
                                term = cpl[a, b, o] * w
                                acc[dz][a] = term if acc[dz][a] is None else acc[dz][a] + term
            for a in range(3):
                before = jnp.where(lane == 0, 0.0, pltpu.roll(acc[0][a], 1, 2))
                after = jnp.where(lane == nz - 1, 0.0, pltpu.roll(acc[2][a], nz - 1, 2))
                out[a, pl.ds(x, step)] = acc[1][a] + before + after

    centre = [cpl[a, a, 13] for a in range(3)]

    for a in range(3):
        scaled = jnp.where(me_failed, 0.0, x_in[a] * stiff[...])
        flat[0, a] = scaled
        pads[0, a, 1:nx + 1, Y0:Y0 + ny, :] = scaled
        inv[a] = 1.0 / (stiff[...] * stiff[...] * centre[a])
    pack(0)

    beside_x = jnp.where(dom > 0, 1, 0) + jnp.where(dom < nd - 1, 1, 0)
    beside_y = jnp.where(bud > 0, 1, 0) + jnp.where(bud < nb - 1, 1, 0)
    pl.semaphore_wait(barrier, nb - 1 + nd - 1 + beside_x * beside_y)

    pieces = [(0, pl.ds(0, nx)), (1, pl.ds(0, 1)), (1, pl.ds(nx - 1, 1)), (1, pl.ds(1, nx - 2))]
    fetch = [[remote(bk.at[w, :, x], saved.at[l, w, :, x], ss.at[l, i], sr.at[l, i], dom, flip(l))
              for l in range(levels)] for i, (w, x) in enumerate(pieces)]
    for i in (1, 2, 3):
        for l in range(levels):
            fetch[i][l].start()
    send_halo(0)
    for l in range(levels):
        fetch[0][l].start()

    keep = [[remote(bsend.at[w], brecv.at[l, w], bs.at[l, w], br.at[l, w], dom, flip(l))
             for l in range(levels)] for w in range(3)]

    def pick(buf, w, a):
        value = buf[0, w, a]
        for l in range(1, levels):
            value = jnp.where(bit_here == l, buf[l, w, a], value)
        return value

    def start_field(x):
        for a in range(3):
            got = saved[0, 1, a, x]
            for l in range(1, levels):
                got = jnp.where(bit_here == l, saved[l, 1, a, x], got)
            p0 = jnp.where(me_failed, got, p_in[a, x])
            bsend[0, a, x] = p0
            u0 = p0 * stiff[x]
            flat[1, a, x] = u0
            pads[1, a, x.start + 1:x.stop + 1, Y0:Y0 + ny, :] = u0

    loads["p"].wait()
    for i in (1, 2):
        for l in range(levels):
            fetch[i][l].wait_recv()
    start_field(slice(0, 1))
    start_field(slice(nx - 1, nx))
    pack(1, True)
    send_halo(1, [s for s in SIDES if s[0] != 0])
    for l in range(levels):
        fetch[3][l].wait_recv()
    start_field(slice(1, nx - 1))
    pack(1, False)
    send_halo(1, [s for s in SIDES if s[0] == 0])
    for l in range(levels):
        keep[0][l].start()
    for name in ("r", "rhs"):
        loads[name].wait()
    for l in range(levels):
        fetch[0][l].wait_recv()
    for a in range(3):
        restored_z = pick(saved, 1, a) - beta[0] * pick(saved, 0, a)
        restored_r = restored_z * (stiff[...] * stiff[...] * centre[a])
        z0 = jnp.where(me_failed, restored_z, inv[a] * r_in[a])
        r0[a] = jnp.where(me_failed, restored_r, r_in[a])
        target[a] = rhs[a] - restored_r
        bsend[1, a] = z0
        a0 = z0 * stiff[...]
        flat[2, a] = a0
        pads[2, a, 1:nx + 1, Y0:Y0 + ny, :] = a0
    pack(2)
    send_halo(2)

    take_halo(1)
    apply(pads.at[1], img.at[0])
    for a in range(3):
        b0 = img[0, a] * (1.0 / jnp.full((1, ny, nz), centre[a], jnp.float32))
        flat[3, a] = b0
        pads[3, a, 1:nx + 1, Y0:Y0 + ny, :] = b0
    pack(3)
    send_halo(3)
    for a in range(3):
        bsend[2, a] = flat[3, a] / stiff[...]
    for w in (1, 2):
        for l in range(levels):
            keep[w][l].start()

    take_halo(2)
    apply(pads.at[2], img.at[1])
    take_halo(0)
    apply(pads.at[0], img3)
    def dot(*terms):
        total = None
        for a in range(3):
            for v in terms:
                t = v(a)
                total = t if total is None else total + t
        return jnp.sum(jnp.sum(total, axis=0), axis=0, keepdims=True)

    red[...] = jnp.zeros(red.shape, red.dtype)
    red[0:1, :] = dot(lambda a: r0[a] * bsend[1, a])
    red[1:2, :] = dot(lambda a: flat[1, a] * img[0, a])
    red[2:3, :] = dot(lambda a: flat[2, a] * img[0, a])
    red[3:4, :] = dot(lambda a: flat[3, a] * img[0, a])
    red[4:5, :] = dot(lambda a: flat[2, a] * img[1, a])
    red[5:6, :] = dot(lambda a: flat[3, a] * img[1, a])
    take_halo(3)
    apply(pads.at[3], img.at[2])
    red[6:7, :] = dot(lambda a: flat[3, a] * img[2, a])

    rows = lax.broadcasted_iota(jnp.int32, (8, nz), 0)
    diagonal = rows == lax.broadcasted_iota(jnp.int32, (8, nz), 1)
    each = jnp.sum(red[...], axis=1, keepdims=True)
    red1[...] = jnp.sum(jnp.where(diagonal, each, 0.0), axis=0, keepdims=True)
    first = [remote(red1, rrecv.at[j - 1], d1s.at[j - 1], d1r.at[j - 1], lax.rem(dom + j, nd), bud)
             for j in range(1, nd)]
    for c in first:
        c.start()

    centre_value = (HIGH + LOW) / 2.0
    half_width = (HIGH - LOW) / 2.0
    ratio_value = centre_value / half_width
    weight = 1.0 / ratio_value
    for a in range(3):
        t = target[a] - img3[a] * stiff[...]
        d = inv[a] * t / centre_value
        target[a] = t
        update[a] = d
        solved[a] = d
        padl[a, 1:nx + 1, Y0:Y0 + ny, :] = d * stiff[...]
    for sweep in range(SWEEPS - 1):
        apply(padl, img3)
        weight_next = 1.0 / (2.0 * ratio_value - weight)
        for a in range(3):
            remain = target[a] - img3[a] * stiff[...]
            d = weight_next * weight * update[a] + (2.0 * weight_next / half_width) * (inv[a] * remain)
            y = solved[a] + d
            update[a] = d
            solved[a] = y
            if sweep < SWEEPS - 2:
                padl[a, 1:nx + 1, Y0:Y0 + ny, :] = y * stiff[...]
        weight = weight_next

    for c in first:
        c.wait_recv()
    total = red1[...]
    for j in range(nd - 1):
        total = total + rrecv[j]
    red2[...] = total
    second = [remote(red2, brecv2.at[j - 1], d2s.at[j - 1], d2r.at[j - 1], dom, lax.rem(bud + j, nb))
              for j in range(1, nb)]
    for c in second:
        c.start()
    for w in range(3):
        for l in range(levels):
            keep[w][l].wait_recv()
    for a in range(3):
        x_out[a] = jnp.where(me_failed, solved[a], x_in[a])
        for w in range(3):
            b_out[w, a] = pick(brecv, w, a)
    s_out[...] = stiff[...]
    for e in range(4):
        end_halo(e)
    for c in second:
        c.wait_recv()
    total = red2[...]
    for j in range(nb - 1):
        total = total + brecv2[j]
    sums = jnp.sum(jnp.where(diagonal, jnp.broadcast_to(total, (8, nz)), 0.0), axis=1, keepdims=True)
    g0, c0, e0, f0, h0, h1, h2 = [jnp.broadcast_to(sums[j:j + 1], (1, nz)) for j in range(7)]
    alpha0 = g0 / c0
    g1 = g0 - 2.0 * alpha0 * e0 + alpha0 * alpha0 * f0
    beta0 = g1 / g0
    c1 = (
        h0 - 2.0 * alpha0 * h1 + alpha0 * alpha0 * h2
        + 2.0 * beta0 * (e0 - alpha0 * f0) + beta0 * beta0 * c0
    )
    alpha1 = g1 / c1
    coef[0:1, :] = alpha0
    coef[1:2, :] = beta0
    coef[2:3, :] = alpha1

    for i in range(4):
        for l in range(levels):
            fetch[i][l].wait_send()
    for w in range(3):
        for l in range(levels):
            keep[w][l].wait_send()
    for c in first + second:
        c.wait_send()


def finish(x0, r0, own, other, img, stiff, coef, x_out, r_out, b_out, xs, rs, bs, sems):
    copies = [pltpu.make_async_copy(other.at[0], b_out.at[0], sems.at[9])]
    copies[0].start()
    alpha0, beta0, alpha1 = coef[0:1, :], coef[1:2, :], coef[2:3, :]
    alpha0, beta0, alpha1 = alpha0[None], beta0[None], alpha1[None]
    for a in range(3):
        bs[a] = other[1, a] - alpha0 * other[2, a] + beta0 * other[0, a]
        p0 = own[0, a]
        p1 = own[1, a] - alpha0 * own[2, a] + beta0 * p0
        xs[a] = x0[a] + alpha0 * p0 + alpha1 * p1
        t0 = img[0, a]
        q1 = img[1, a] - alpha0 * img[2, a] + beta0 * t0
        rs[a] = r0[a] - stiff[...] * (alpha0 * t0 + alpha1 * q1)
        for i, (src, dst) in enumerate((
            (bs.at[a], b_out.at[1, a]), (xs.at[a], x_out.at[a]), (rs.at[a], r_out.at[a]),
        )):
            copies.append(pltpu.make_async_copy(src, dst, sems.at[a * 3 + i]))
            copies[-1].start()
    for c in copies:
        c.wait()


def on_device(nd, nb, rhs, stiff, coupling, x_in, r_in, p_in, backup_in, beta, fc, bb):
    levels = nb.bit_length() - 1
    nx, ny, nz = stiff.shape
    f32 = jnp.float32
    rows = -(-3 * nx // 8) * 8
    vmem = pl.BlockSpec(memory_space=pltpu.VMEM)
    smem = pl.BlockSpec(memory_space=pltpu.SMEM)
    hbm = pl.BlockSpec(memory_space=pltpu.HBM)
    field = (3, nx, ny, nz)
    dma = pltpu.SemaphoreType.DMA
    parts = pl.pallas_call(
        functools.partial(kernel, nd, nb, levels),
        out_shape=(
            pltpu.VMEM(field, f32),
            pltpu.VMEM(field, f32),
            pltpu.VMEM((3,) + field, f32),
            pltpu.VMEM((3,) + field, f32),
            pltpu.VMEM((3,) + field, f32),
            pltpu.VMEM((nx, ny, nz), f32),
            pltpu.VMEM((8, nz), f32),
        ),
        in_specs=[hbm] * 7 + [smem] * 3,
        out_specs=(vmem,) * 7,
        scratch_shapes=[
            pltpu.VMEM(field, f32),
            pltpu.VMEM((nx, ny, nz), f32),
            pltpu.SMEM((3, 3, 27), f32),
            pltpu.VMEM(field, f32),
            pltpu.VMEM(field, f32),
            pltpu.VMEM(field, f32),
            dma((6,)),
            pltpu.VMEM((4, 3, nx + 2, ny + 2 * Y0, nz), f32),
            pltpu.VMEM((3, nx + 2, ny + 2 * Y0, nz), f32),
            pltpu.VMEM((4,) + field, f32),
            pltpu.VMEM((4, 2, rows, nz), f32),
            pltpu.VMEM((4, 2, rows, nz), f32),
            pltpu.VMEM((4, 8, 8, nz), f32),
            pltpu.VMEM((4, 8, 8, nz), f32),
            pltpu.VMEM((levels, 2) + field, f32),
            pltpu.VMEM((levels, 3) + field, f32),
            pltpu.VMEM(field, f32),
            pltpu.VMEM(field, f32),
            pltpu.VMEM(field, f32),
            pltpu.VMEM(field, f32),
            pltpu.VMEM(field, f32),
            pltpu.VMEM((8, nz), f32),
            pltpu.VMEM((1, nz), f32),
            pltpu.VMEM((1, nz), f32),
            pltpu.VMEM((nd - 1, 1, nz), f32),
            pltpu.VMEM((nb - 1, 1, nz), f32),
            dma((4, 8)), dma((4, 8)),
            dma((levels, 4)), dma((levels, 4)),
            dma((levels, 3)), dma((levels, 3)),
            dma((nd - 1,)), dma((nd - 1,)),
            dma((nb - 1,)), dma((nb - 1,)),
        ],
        compiler_params=pltpu.CompilerParams(
            collective_id=0, has_side_effects=True, vmem_limit_bytes=40 * 1024 * 1024
        ),
    )(*[pltpu.with_memory_space_constraint(v, pltpu.HBM) for v in (
        rhs, stiff, jnp.transpose(coupling, (1, 2, 0)), x_in, r_in, p_in, backup_in
    )], beta, fc, bb)
    return pl.pallas_call(
        finish,
        out_shape=(
            pltpu.HBM(field, f32), pltpu.HBM(field, f32), pltpu.HBM((2,) + field, f32),
        ),
        in_specs=[vmem] * 7,
        out_specs=(hbm, hbm, hbm),
        scratch_shapes=[
            pltpu.VMEM(field, f32), pltpu.VMEM(field, f32), pltpu.VMEM(field, f32), dma((10,)),
        ],
        compiler_params=pltpu.CompilerParams(vmem_limit_bytes=8 * 1024 * 1024),
    )(*parts)


def solution(mesh):
    nd, nb = mesh.shape["dom"], mesh.shape["bud"]
    placed = (
        P(None, "dom", "bud", None),
        P("dom", "bud", None),
        P(),
        P(None, "dom", "bud", None),
        P(None, "dom", "bud", None),
        P(None, "dom", "bud", None),
        P(None, None, "dom", "bud", None),
        P(),
        P("dom"),
        P("dom"),
    )
    return jax.shard_map(
        functools.partial(on_device, nd, nb),
        mesh=mesh,
        in_specs=placed,
        out_specs=(
            P(None, "dom", "bud", None),
            P(None, "dom", "bud", None),
            P(None, None, "dom", "bud", None),
        ),
        check_vma=False,
    )
```

profile of v0, /device:TPU:0, one launch (start us, length us, event | category | flops | bytes accessed | tf_op | source)
XLA Modules:
  0.0 29.3 jit_solution(15009456051717485711)
XLA Ops:
  2.6 25.9 %shard_map.121 = (f32[3,4,16,128]{3,2,1,0:T(8,128)S(1)}, f32[3,4,16,128]{3,2,1,0:T(8,128)S(1)}, f32[3,3,4,16,128]{4,3,2,1,0:T(8,128)S(1)}, f32[3,3,4,16,128]{4,3...) custom-call(f32[3,4,16,128]{3,2,1,0:T(8,128)} %rhs_h.1, ...), custom_call_target="tpu_custom_call" | custom-call | tf_op jit(solution)/shard_map/pallas_call | solution.py:408
  28.5 0.8 %shard_map.122 = (f32[3,4,16,128]{3,2,1,0:T(8,128)}, f32[3,4,16,128]{3,2,1,0:T(8,128)}, f32[2,3,4,16,128]{4,3,2,1,0:T(8,128)}) custom-call(f32[3,4,16,128]{3,2,1,0:T(8,128)S(1)} %get-tuple-element.10.x0, f32[3,4,16,128]{3,2,1,0:T(8,128)S(1)} %get-tuple-element.11.r0, f32[3,3,4,16,128]{4,3,2,1,0:T(8,128)S(1)} %get-tuple-element.12.own, ...), custom_call_target="tpu_custom_call" | custom-call | tf_op jit(solution)/shard_map/pallas_call | solution.py:460
where the time goes:
time: 29.5 us; the launch traced here: 29.3 us
  Pallas kernels  26.7 us (91%)
  between operations  2.58 us (9%)
    pallas_call x1, Pallas kernels, on_device(): pl.pallas_call(functools.partial(kernel, nd, nb, levels), out_shape=(pltp...  25.9 us
    pallas_call x1, Pallas kernels, on_device(): pl.pallas_call(finish, out_shape=(pltpu.HBM(field, f32), pltpu.HBM(field,...  0.82 us

commit v1 on v0

--- a/solution.py
+++ b/solution.py
@@ -16,13 +16,13 @@
 
 def kernel(
     nd, nb, levels,
-    rhs_h, stiff_h, cpl_h, x_h, r_h, p_h, bk, beta, fc, bb,
+    rhs_h, stiff_h, cpl_h, x_h, r_h, p_h, bk, beta_h, fc_h, bb_h,
     x_out, r0, bsend, b_out, img, s_out, coef,
-    rhs, stiff, cpl, x_in, r_in, p_in, in_sems,
+    rhs, stiff, cpl, x_in, r_in, p_in, beta, fc, bb, in_sems,
     pads, padl, flat, ysend, yrecv, csend, crecv, saved, brecv,
     inv, img3, target, solved, update,
-    red, red1, red2, rrecv, brecv2,
-    hs, hr, ss, sr, bs, br, d1s, d1r, d2s, d2r,
+    red, red1, rall,
+    hs, hr, ss, sr, bs, br, ds, dr, know,
 ):
     nx, ny, nz = stiff.shape
     step = 2 if nx % 2 == 0 else 1
@@ -48,10 +48,37 @@
         stride = 1 << level
         return bud + stride * (1 - 2 * (lax.rem(bud // stride, 2)))
 
+    barrier = pltpu.get_barrier_semaphore()
+
+    def greet(sem, d, b):
+        pl.semaphore_signal(
+            sem, inc=1, device_id={"dom": d, "bud": b},
+            device_id_type=pl.DeviceIdType.MESH,
+        )
+
+    def ahead(stride):
+        return jnp.where(dom >= stride, 1, 0) + jnp.where(dom < nd - stride, 1, 0)
+
+    def greet_dom(sem, stride):
+        @pl.when(dom >= stride)
+        def _():
+            greet(sem, dom - stride, bud)
+
+        @pl.when(dom < nd - stride)
+        def _():
+            greet(sem, dom + stride, bud)
+
+    def greet_near(sem):
+        greet_dom(sem, 1)
+        for j in range(1, nb):
+            greet(sem, dom, lax.rem(bud + j, nb))
+
+    strides = [1 << i for i in range(max(nd - 1, 1).bit_length())]
     coef[...] = jnp.zeros(coef.shape, coef.dtype)
     loads = {}
     for i, (name, src, dst) in enumerate((
-        ("cpl", cpl_h, cpl), ("stiff", stiff_h, stiff), ("x", x_h, x_in),
+        ("cpl", cpl_h, cpl), ("fc", fc_h, fc), ("bb", bb_h, bb), ("beta", beta_h, beta),
+        ("stiff", stiff_h, stiff), ("x", x_h, x_in),
         ("p", p_h, p_in), ("r", r_h, r_in), ("rhs", rhs_h, rhs),
     )):
         loads[name] = pltpu.make_async_copy(src, dst, in_sems.at[i])
@@ -66,26 +93,9 @@
         pad[:, 1:nx + 1, Y0 + ny:ny + 2 * Y0, :] = rim
     yrecv[...] = jnp.zeros(yrecv.shape, yrecv.dtype)
     crecv[...] = jnp.zeros(crecv.shape, crecv.dtype)
-
-    barrier = pltpu.get_barrier_semaphore()
-
-    def greet(d, b):
-        pl.semaphore_signal(
-            barrier, inc=1, device_id={"dom": d, "bud": b},
-            device_id_type=pl.DeviceIdType.MESH,
-        )
-
-    for j in range(1, nb):
-        greet(dom, lax.rem(bud + j, nb))
-    for j in range(1, nd):
-        greet(lax.rem(dom + j, nd), bud)
-    diagonals = [s for s in SIDES if s[0] != 0 and s[1] != 0]
-    for side in diagonals:
-        @pl.when(has(side))
-        def _(side=side):
-            greet(dom + side[0], bud + side[1])
-
-    for name in ("cpl", "stiff", "x"):
+    greet_near(barrier)
+
+    for name in ("cpl", "fc", "bb", "stiff", "x"):
         loads[name].wait()
     me_failed = jnp.full((1, ny, nz), fc[0], jnp.int32) == bud
     bit_here = jnp.full((1, ny, nz), bb[0], jnp.int32)
@@ -188,9 +198,8 @@
         inv[a] = 1.0 / (stiff[...] * stiff[...] * centre[a])
     pack(0)
 
-    beside_x = jnp.where(dom > 0, 1, 0) + jnp.where(dom < nd - 1, 1, 0)
-    beside_y = jnp.where(bud > 0, 1, 0) + jnp.where(bud < nb - 1, 1, 0)
-    pl.semaphore_wait(barrier, nb - 1 + nd - 1 + beside_x * beside_y)
+    pl.semaphore_wait(barrier, nb - 1 + ahead(1))
+    greet_near(know.at[0])
 
     pieces = [(0, pl.ds(0, nx)), (1, pl.ds(0, 1)), (1, pl.ds(nx - 1, 1)), (1, pl.ds(1, nx - 2))]
     fetch = [[remote(bk.at[w, :, x], saved.at[l, w, :, x], ss.at[l, i], sr.at[l, i], dom, flip(l))
@@ -198,9 +207,13 @@
     for i in (1, 2, 3):
         for l in range(levels):
             fetch[i][l].start()
-    send_halo(0)
+    send_halo(0, [s for s in SIDES if s[0] == 0 or s[1] == 0])
     for l in range(levels):
         fetch[0][l].start()
+    pl.semaphore_wait(know.at[0], nb - 1 + ahead(1))
+    for i, stride in enumerate(strides[1:2]):
+        greet_dom(know.at[1], stride)
+    send_halo(0, [s for s in SIDES if s[0] != 0 and s[1] != 0])
 
     keep = [[remote(bsend.at[w], brecv.at[l, w], bs.at[l, w], br.at[l, w], dom, flip(l))
              for l in range(levels)] for w in range(3)]
@@ -237,7 +250,11 @@
     send_halo(1, [s for s in SIDES if s[0] == 0])
     for l in range(levels):
         keep[0][l].start()
-    for name in ("r", "rhs"):
+    for i in range(1, len(strides)):
+        pl.semaphore_wait(know.at[i], ahead(strides[i]))
+        if i + 1 < len(strides):
+            greet_dom(know.at[i + 1], strides[i + 1])
+    for name in ("r", "rhs", "beta"):
         loads[name].wait()
     for l in range(levels):
         fetch[0][l].wait_recv()
@@ -295,10 +312,17 @@
     diagonal = rows == lax.broadcasted_iota(jnp.int32, (8, nz), 1)
     each = jnp.sum(red[...], axis=1, keepdims=True)
     red1[...] = jnp.sum(jnp.where(diagonal, each, 0.0), axis=0, keepdims=True)
-    first = [remote(red1, rrecv.at[j - 1], d1s.at[j - 1], d1r.at[j - 1], lax.rem(dom + j, nd), bud)
-             for j in range(1, nd)]
-    for c in first:
-        c.start()
+    n = nd * nb
+    me = dom * nb + bud
+    rall[me] = red1[...]
+    order = sorted(range(1, n), key=lambda j: abs(2 * j - n))
+    for j in order:
+        peer = lax.rem(me + j, n)
+        remote(red1, rall.at[me], ds.at[0], dr.at[0], peer // nb, lax.rem(peer, nb)).start()
+
+    def every():
+        part = rall.at[pl.ds(0, n - 1)]
+        return remote(part, part, ds.at[0], dr.at[0], dom, bud)
 
     centre_value = (HIGH + LOW) / 2.0
     half_width = (HIGH - LOW) / 2.0
@@ -324,16 +348,6 @@
                 padl[a, 1:nx + 1, Y0:Y0 + ny, :] = y * stiff[...]
         weight = weight_next
 
-    for c in first:
-        c.wait_recv()
-    total = red1[...]
-    for j in range(nd - 1):
-        total = total + rrecv[j]
-    red2[...] = total
-    second = [remote(red2, brecv2.at[j - 1], d2s.at[j - 1], d2r.at[j - 1], dom, lax.rem(bud + j, nb))
-              for j in range(1, nb)]
-    for c in second:
-        c.start()
     for w in range(3):
         for l in range(levels):
             keep[w][l].wait_recv()
@@ -344,11 +358,8 @@
     s_out[...] = stiff[...]
     for e in range(4):
         end_halo(e)
-    for c in second:
-        c.wait_recv()
-    total = red2[...]
-    for j in range(nb - 1):
-        total = total + brecv2[j]
+    every().wait_recv()
+    total = jnp.sum(rall[...], axis=0)
     sums = jnp.sum(jnp.where(diagonal, jnp.broadcast_to(total, (8, nz)), 0.0), axis=1, keepdims=True)
     g0, c0, e0, f0, h0, h1, h2 = [jnp.broadcast_to(sums[j:j + 1], (1, nz)) for j in range(7)]
     alpha0 = g0 / c0
@@ -369,8 +380,7 @@
     for w in range(3):
         for l in range(levels):
             keep[w][l].wait_send()
-    for c in first + second:
-        c.wait_send()
+    every().wait_send()
 
 
 def finish(x0, r0, own, other, img, stiff, coef, x_out, r_out, b_out, xs, rs, bs, sems):
@@ -401,7 +411,6 @@
     f32 = jnp.float32
     rows = -(-3 * nx // 8) * 8
     vmem = pl.BlockSpec(memory_space=pltpu.VMEM)
-    smem = pl.BlockSpec(memory_space=pltpu.SMEM)
     hbm = pl.BlockSpec(memory_space=pltpu.HBM)
     field = (3, nx, ny, nz)
     dma = pltpu.SemaphoreType.DMA
@@ -416,7 +425,7 @@
             pltpu.VMEM((nx, ny, nz), f32),
             pltpu.VMEM((8, nz), f32),
         ),
-        in_specs=[hbm] * 7 + [smem] * 3,
+        in_specs=[hbm] * 7 + [pl.BlockSpec(memory_space=pl.ANY)] * 3,
         out_specs=(vmem,) * 7,
         scratch_shapes=[
             pltpu.VMEM(field, f32),
@@ -425,7 +434,10 @@
             pltpu.VMEM(field, f32),
             pltpu.VMEM(field, f32),
             pltpu.VMEM(field, f32),
-            dma((6,)),
+            pltpu.SMEM((1,), f32),
+            pltpu.SMEM((1,), jnp.int32),
+            pltpu.SMEM((1,), jnp.int32),
+            dma((9,)),
             pltpu.VMEM((4, 3, nx + 2, ny + 2 * Y0, nz), f32),
             pltpu.VMEM((3, nx + 2, ny + 2 * Y0, nz), f32),
             pltpu.VMEM((4,) + field, f32),
@@ -442,14 +454,12 @@
             pltpu.VMEM(field, f32),
             pltpu.VMEM((8, nz), f32),
             pltpu.VMEM((1, nz), f32),
-            pltpu.VMEM((1, nz), f32),
-            pltpu.VMEM((nd - 1, 1, nz), f32),
-            pltpu.VMEM((nb - 1, 1, nz), f32),
+            pltpu.VMEM((nd * nb, 1, nz), f32),
             dma((4, 8)), dma((4, 8)),
             dma((levels, 4)), dma((levels, 4)),
             dma((levels, 3)), dma((levels, 3)),
-            dma((nd - 1,)), dma((nd - 1,)),
-            dma((nb - 1,)), dma((nb - 1,)),
+            dma((1,)), dma((1,)),
+            pltpu.SemaphoreType.REGULAR((nd.bit_length(),)),
         ],
         compiler_params=pltpu.CompilerParams(
             collective_id=0, has_side_effects=True, vmem_limit_bytes=40 * 1024 * 1024

time: 29.5 us -> 27.2 us (0.922)
  Pallas kernels: 26.7 us -> 24.4 us
    pallas_call x1, Pallas kernels: 25.9 us -> 23.6 us  [on_device(): pl.pallas_call(functools.partial(kernel, nd, nb, levels), out_shape=(pltp...]
where the time goes in v1:
time: 27.2 us; the launch traced here: 27 us
  Pallas kernels  24.4 us (90%)
  between operations  2.58 us (9%)
    pallas_call x1, Pallas kernels, on_device(): pl.pallas_call(functools.partial(kernel, nd, nb, levels), out_shape=(pltp...  23.6 us
    pallas_call x1, Pallas kernels, on_device(): pl.pallas_call(finish, out_shape=(pltpu.HBM(field, f32), pltpu.HBM(field,...  0.82 us

profile of v1, /device:TPU:0, one launch (start us, length us, event | category | flops | bytes accessed | tf_op | source)
XLA Modules:
  0.0 27.0 jit_solution(1289740839570262660)
XLA Ops:
  2.6 23.6 %shard_map.121 = (f32[3,4,16,128]{3,2,1,0:T(8,128)S(1)}, f32[3,4,16,128]{3,2,1,0:T(8,128)S(1)}, f32[3,3,4,16,128]{4,3,2,1,0:T(8,128)S(1)}, f32[3,3,4,16,128]{4,3...) custom-call(f32[3,4,16,128]{3,2,1,0:T(8,128)} %rhs_h.1, ...), custom_call_target="tpu_custom_call" | custom-call | tf_op jit(solution)/shard_map/pallas_call | solution.py:417
  26.2 0.8 %shard_map.122 = (f32[3,4,16,128]{3,2,1,0:T(8,128)}, f32[3,4,16,128]{3,2,1,0:T(8,128)}, f32[2,3,4,16,128]{4,3,2,1,0:T(8,128)}) custom-call(f32[3,4,16,128]{3,2,1,0:T(8,128)S(1)} %get-tuple-element.10.x0, f32[3,4,16,128]{3,2,1,0:T(8,128)S(1)} %get-tuple-element.11.r0, f32[3,3,4,16,128]{4,3,2,1,0:T(8,128)S(1)} %get-tuple-element.12.own, ...), custom_call_target="tpu_custom_call" | custom-call | tf_op jit(solution)/shard_map/pallas_call | solution.py:470

commit v2 on v1

v2 whole, which is shorter than its diff:
```python
import functools

import jax
import jax.numpy as jnp
from jax import lax
from jax.experimental import pallas as pl
from jax.experimental.pallas import tpu as pltpu
from jax.sharding import PartitionSpec as P

SWEEPS = 4
LOW = 0.01
HIGH = 1.99
Y0 = 8
CORNERS = [(sx, sy) for sx in (-1, 1) for sy in (-1, 1)]


class Halo:
    def __init__(self, depth, pad, ysend, yrecv, csend, crecv, send, recv):
        self.depth, self.pad = depth, pad
        self.ysend, self.yrecv, self.csend, self.crecv = ysend, yrecv, csend, crecv
        self.send, self.recv = send, recv


def halo_sems(depth):
    return 6 * depth + 2


def kernel(
    nd, nb, levels,
    rhs_h, stiff_h, cpl_h, x_h, r_h, p_h, bk_h, beta, fc, bb,
    x_out, r0, own, other, img, s_out, coef,
    rhs, stiff, cpl, x_in, r_in, p_in, bk, in_sems,
    upad, apad, xpad, bpad, lpad,
    yus, yur, cus, cur, yas, yar, cas, car, yxs, yxr, cxs, cxr,
    edge, edge_out, saved, brecv,
    inv, invs, img3, target, solved, update,
    red, red1, rall,
    us, ur, as_, ar, xs, xr, ss, sr, bs, br, ds, dr, know,
):
    nx, ny, nz = stiff.shape
    step = 2 if nx % 2 == 0 else 1
    dom, bud = lax.axis_index("dom"), lax.axis_index("bud")
    f32 = jnp.float32

    def has(sx, sy):
        ok = None
        for cond in (
            ([dom > 0] if sx < 0 else [dom < nd - 1] if sx > 0 else [])
            + ([bud > 0] if sy < 0 else [bud < nb - 1] if sy > 0 else [])
        ):
            ok = cond if ok is None else jnp.logical_and(ok, cond)
        return ok

    def remote(src, dst, send, recv, d, b):
        return pltpu.make_async_remote_copy(
            src_ref=src, dst_ref=dst, send_sem=send, recv_sem=recv,
            device_id={"dom": d, "bud": b}, device_id_type=pl.DeviceIdType.MESH,
        )

    def flip(level):
        stride = 1 << level
        return bud + stride * (1 - 2 * (lax.rem(bud // stride, 2)))

    barrier = pltpu.get_barrier_semaphore()

    def greet(sem, d, b):
        pl.semaphore_signal(
            sem, inc=1, device_id={"dom": d, "bud": b},
            device_id_type=pl.DeviceIdType.MESH,
        )

    def ahead(stride):
        return jnp.where(dom >= stride, 1, 0) + jnp.where(dom < nd - stride, 1, 0)

    def greet_dom(sem, stride):
        @pl.when(dom >= stride)
        def _():
            greet(sem, dom - stride, bud)

        @pl.when(dom < nd - stride)
        def _():
            greet(sem, dom + stride, bud)

    def greet_near(sem):
        greet_dom(sem, 1)
        for j in range(1, nb):
            greet(sem, dom, lax.rem(bud + j, nb))

    strides = [1 << i for i in range(max(nd - 1, 1).bit_length())]
    greet_near(barrier)

    loads = {}
    for i, (name, src, dst) in enumerate((
        ("cpl", cpl_h, cpl), ("bk", bk_h, bk), ("stiff", stiff_h, stiff), ("x", x_h, x_in),
        ("p", p_h, p_in), ("r", r_h, r_in), ("rhs", rhs_h, rhs),
    )):
        loads[name] = pltpu.make_async_copy(src, dst, in_sems.at[i])
        loads[name].start()

    U = Halo(2, upad, yus, yur, cus, cur, us, ur)
    A = Halo(1, apad, yas, yar, cas, car, as_, ar)
    X = Halo(1, xpad, yxs, yxr, cxs, cxr, xs, xr)
    inner = pl.ds(Y0, ny)

    for h in (U, A, X):
        deep = h.depth
        for sx in (-1, 1):
            @pl.when(jnp.logical_not(has(sx, 0)))
            def _(h=h, deep=deep, sx=sx):
                for d in range(deep):
                    x = deep - 1 - d if sx < 0 else deep + nx + d
                    h.pad[:, x, inner, :] = jnp.zeros((3, ny, nz), f32)

        for sy in (-1, 1):
            @pl.when(jnp.logical_not(has(0, sy)))
            def _(h=h, sy=sy):
                i = 1 if sy > 0 else 0
                h.yrecv[i] = jnp.zeros(h.yrecv.shape[1:], f32)

        for q, (sx, sy) in enumerate(CORNERS):
            @pl.when(jnp.logical_not(has(sx, sy)))
            def _(h=h, q=q):
                h.crecv[q] = jnp.zeros(h.crecv.shape[1:], f32)

    def xface(h, sx, d):
        deep = h.depth
        src = deep + (nx - 1 - d if sx > 0 else d)
        dst = deep - 1 - d if sx > 0 else deep + nx + d
        i, o = (deep + d, d) if sx > 0 else (d, deep + d)
        return remote(
            h.pad.at[:, src, inner, :], h.pad.at[:, dst, inner, :],
            h.send.at[i], h.recv.at[o], dom + sx, bud,
        )

    def yface(h, sy):
        i, o = (1, 0) if sy > 0 else (0, 1)
        return remote(
            h.ysend.at[i], h.yrecv.at[o],
            h.send.at[2 * h.depth + i], h.recv.at[2 * h.depth + o], dom, bud + sy,
        )

    def corner(h, q, e):
        sx, sy = CORNERS[q]
        base = 2 * h.depth + 2
        return remote(
            h.csend.at[q, e], h.crecv.at[3 - q, e],
            h.send.at[base + q * h.depth + e], h.recv.at[base + (3 - q) * h.depth + e],
            dom + sx, bud + sy,
        )

    def xland(h, sx, d):
        deep = h.depth
        x = deep + nx + d if sx > 0 else deep - 1 - d
        i = deep + d if sx > 0 else d
        part = h.pad.at[:, x, inner, :]
        return remote(part, part, h.send.at[i], h.recv.at[i], dom + sx, bud)

    def yland(h, sy):
        i = 1 if sy > 0 else 0
        part = h.yrecv.at[i]
        return remote(part, part, h.send.at[2 * h.depth + i], h.recv.at[2 * h.depth + i], dom, bud + sy)

    def cland(h, q, e):
        sx, sy = CORNERS[q]
        i = 2 * h.depth + 2 + q * h.depth + e
        part = h.crecv.at[q, e]
        return remote(part, part, h.send.at[i], h.recv.at[i], dom + sx, bud + sy)

    def each_x(h, d, do):
        for sx in (-1, 1):
            @pl.when(has(sx, 0))
            def _(sx=sx):
                do(h, sx, d)

    def each_y(h, do):
        for sy in (-1, 1):
            @pl.when(has(0, sy))
            def _(sy=sy):
                do(h, sy)

    def each_c(h, e, do):
        for q, (sx, sy) in enumerate(CORNERS):
            @pl.when(has(sx, sy))
            def _(q=q):
                do(h, q, e)

    def pack_y(h):
        deep = h.depth
        for i in range(2):
            for b in range(3):
                for d in range(deep):
                    y = Y0 + (ny - deep + d if i else d)
                    for x in range(nx):
                        h.ysend[i, b, d, x:x + 1, :] = h.pad[b, deep + x, y:y + 1, :]

    def pack_c(h, e):
        deep = h.depth
        for q, (sx, sy) in enumerate(CORNERS):
            x = deep + (nx - 1 - e if sx > 0 else e)
            for b in range(3):
                for d in range(deep):
                    y = Y0 + (ny - deep + d if sy > 0 else d)
                    h.csend[q, e, b, d:d + 1, :] = h.pad[b, x, y:y + 1, :]

    def unpack_y(h):
        deep = h.depth
        for i in range(2):
            y, d = (Y0 + ny, 0) if i else (Y0 - 1, deep - 1)
            for b in range(3):
                for x in range(nx):
                    h.pad[b, deep + x, y:y + 1, :] = h.yrecv[i, b, d, x:x + 1, :]

    def unpack_c(h, e):
        deep = h.depth
        for q, (sx, sy) in enumerate(CORNERS):
            x = deep + nx + e if sx > 0 else deep - 1 - e
            y, d = (Y0 + ny, 0) if sy > 0 else (Y0 - 1, deep - 1)
            for b in range(3):
                h.pad[b, x, y:y + 1, :] = h.crecv[q, e, b, d:d + 1, :]

    def start_x(h, d):
        each_x(h, d, lambda *a: xface(*a).start())

    def start_y(h):
        each_y(h, lambda *a: yface(*a).start())

    def start_c(h, e):
        each_c(h, e, lambda *a: corner(*a).start())

    def take(h, d):
        each_x(h, d, lambda *a: xland(*a).wait_recv())
        each_c(h, d, lambda *a: cland(*a).wait_recv())
        if d == 0:
            each_y(h, lambda *a: yland(*a).wait_recv())
            unpack_y(h)
        unpack_c(h, d)

    def end(h):
        for d in range(h.depth):
            each_x(h, d, lambda *a: xface(*a).wait_send())
            each_c(h, d, lambda *a: corner(*a).wait_send())
        each_y(h, lambda *a: yface(*a).wait_send())

    def stencil(load, groups):
        acc = [[[None] * groups for _ in range(3)] for _ in range(3)]
        for dx in range(3):
            for dy in range(3):
                for b in range(3):
                    ws = [load(b, dx, dy, g) for g in range(groups)]
                    for dz in range(3):
                        o = (dx * 3 + dy) * 3 + dz
                        for a in range(3):
                            for g in range(groups):
                                term = cpl[a, b, o] * ws[g]
                                old = acc[dz][a][g]
                                acc[dz][a][g] = term if old is None else old + term
        lane = lax.broadcasted_iota(jnp.int32, acc[0][0][0].shape, 1)

        def joined(a, g):
            before = jnp.where(lane == 0, 0.0, pltpu.roll(acc[0][a][g], 1, 1))
            after = jnp.where(lane == nz - 1, 0.0, pltpu.roll(acc[2][a][g], nz - 1, 1))
            return acc[1][a][g] + before + after

        return [[joined(a, g) for g in range(groups)] for a in range(3)]

    def apply(pad, deep, out):
        @pl.loop(0, nx // step)
        def _(j):
            x = j * step
            got = stencil(
                lambda b, dx, dy, g: pad[b, x + (g + deep - 1 + dx), Y0 - 1 + dy:Y0 - 1 + dy + ny, :], step
            )
            for a in range(3):
                for g in range(step):
                    out[a, x + g] = got[a][g]

    for name in ("cpl", "stiff", "x", "bk"):
        loads[name].wait()
    me_failed = jnp.full((1, ny, nz), fc[0], jnp.int32) == bud
    bit_here = jnp.full((1, ny, nz), bb[0], jnp.int32)
    centre = [cpl[a, a, 13] for a in range(3)]
    for a in range(3):
        xpad[a, 1:nx + 1, inner, :] = jnp.where(me_failed, 0.0, x_in[a] * stiff[...])
    pack_y(X)
    pack_c(X, 0)

    pl.semaphore_wait(barrier, nb - 1 + ahead(1))

    pieces = [pl.ds(0, 1), pl.ds(nx - 1, 1), pl.ds(1, nx - 2)]
    fetch = [[[remote(bk.at[w, :, x], saved.at[l, w, :, x], ss.at[l, w, i], sr.at[l, w, i], dom, flip(l))
               for l in range(levels)] for i, x in enumerate(pieces)] for w in range(2)]
    for w in (1, 0):
        for i in range(3):
            for l in range(levels):
                fetch[w][i][l].start()
    greet_near(know.at[0])
    start_x(X, 0)
    start_y(X)

    coef[...] = jnp.zeros(coef.shape, f32)
    red[...] = jnp.zeros(red.shape, f32)
    for x in (0, nx + 1):
        lpad[:, x] = jnp.zeros((3, ny + 2 * Y0, nz), f32)
    for y in (0, Y0 + ny):
        lpad[:, 1:nx + 1, y:y + Y0, :] = jnp.zeros((3, nx, Y0, nz), f32)
    invs[...] = 1.0 / stiff[...]
    inv_centre = [1.0 / jnp.full((1, nz), centre[a], f32) for a in range(3)]
    for a in range(3):
        inv[a] = 1.0 / (stiff[...] * stiff[...] * centre[a])

    pl.semaphore_wait(know.at[0], nb - 1 + ahead(1))
    if len(strides) > 1:
        greet_dom(know.at[1], strides[1])
    start_c(X, 0)

    def pick(value, l_of):
        got = l_of(0)
        for l in range(1, levels):
            got = jnp.where(bit_here == l, l_of(l), got)
        return jnp.where(me_failed, got, value)

    def start_field(x):
        for a in range(3):
            p0 = pick(p_in[a, x], lambda l: saved[l, 1, a, x])
            own[0, a, x] = p0
            upad[a, x.start + 2:x.stop + 2, inner, :] = p0 * stiff[x]

    loads["p"].wait()
    for i in (0, 1):
        for l in range(levels):
            fetch[1][i][l].wait_recv()
    start_field(slice(0, 1))
    start_field(slice(nx - 1, nx))
    pack_c(U, 0)
    start_c(U, 0)
    start_x(U, 0)
    for l in range(levels):
        fetch[1][2][l].wait_recv()
    start_field(slice(1, nx - 1))
    pack_c(U, 1)
    start_c(U, 1)
    start_x(U, 1)
    pack_y(U)
    start_y(U)

    keep = [[[remote(own.at[w, :, x], brecv.at[l, w, :, x], bs.at[l, w, i], br.at[l, w, i], dom, flip(l))
              for l in range(levels)] for i, x in enumerate((pl.ds(0, nx // 2), pl.ds(nx // 2, nx - nx // 2)))]
            for w in range(3)]

    def start_keep(w, i):
        for l in range(levels):
            keep[w][i][l].start()

    start_keep(0, 0)
    for i in range(1, len(strides)):
        pl.semaphore_wait(know.at[i], ahead(strides[i]))
        if i + 1 < len(strides):
            greet_dom(know.at[i + 1], strides[i + 1])

    def second_field(x):
        for a in range(3):
            s = stiff[x]
            restored_z = pick(0.0, lambda l: saved[l, 1, a, x]) - beta[0] * pick(0.0, lambda l: saved[l, 0, a, x])
            restored_r = restored_z * (s * s * centre[a])
            z0 = jnp.where(me_failed, restored_z, inv[a, x] * r_in[a, x])
            r0[a, x] = jnp.where(me_failed, restored_r, r_in[a, x])
            target[a, x] = rhs[a, x] - restored_r
            own[1, a, x] = z0
            apad[a, x.start + 1:x.stop + 1, inner, :] = z0 * s

    for name in ("r", "rhs"):
        loads[name].wait()
    for i in (0, 1):
        for l in range(levels):
            fetch[0][i][l].wait_recv()
    second_field(slice(0, 1))
    second_field(slice(nx - 1, nx))
    pack_c(A, 0)
    start_c(A, 0)
    start_x(A, 0)
    for l in range(levels):
        fetch[0][2][l].wait_recv()
    second_field(slice(1, nx - 1))
    pack_y(A)
    start_y(A)
    start_keep(0, 1)
    start_keep(1, 0)
    start_keep(1, 1)

    take(U, 0)
    apply(upad, 2, img.at[0])
    for a in range(3):
        b0 = img[0, a] * inv_centre[a]
        bpad[a, 1:nx + 1, inner, :] = b0
        own[2, a] = b0 * invs[...]
    take(U, 1)
    for b in range(3):
        for i in range(2):
            for d in range(2):
                lev = i + d
                edge[i, b, lev, 2:nx + 2, :] = yur[i, b, d]
                for q, (sx, sy) in enumerate(CORNERS):
                    if (sy > 0) == bool(i):
                        for e in range(2):
                            x = nx + 2 + e if sx > 0 else 1 - e
                            edge[i, b, lev, x:x + 1, :] = cur[q, e, b, d:d + 1, :]
            y = Y0 + (ny - 1 if i else 0)
            for x in range(nx + 4):
                edge[i, b, 0 if i else 2, x:x + 1, :] = upad[b, x, y:y + 1, :]

    rim = stencil(lambda b, dx, dy, g: upad[b, (nx + 1 if g else 0) + dx, Y0 - 1 + dy:Y0 - 1 + dy + ny, :], 2)
    for a in range(3):
        for g, sx in enumerate((-1, 1)):
            b0 = rim[a][g] * inv_centre[a]
            bpad[a, nx + 1 if g else 0, inner, :] = jnp.where(has(sx, 0), b0, 0.0)
    rim = stencil(lambda b, dx, dy, g: edge[g, b, dy, dx:dx + nx + 2, :], 2)
    row = lax.broadcasted_iota(jnp.int32, (nx + 2, nz), 0)
    first_in = jnp.where(dom > 0, 0, 1)
    last_in = jnp.where(dom < nd - 1, nx + 1, nx)
    inside = jnp.logical_and(row >= first_in, row <= last_in)
    for a in range(3):
        for g, sy in enumerate((-1, 1)):
            b0 = jnp.where(inside, rim[a][g] * inv_centre[a], 0.0)
            edge_out[g, a, 0:nx + 2, :] = jnp.where(has(0, sy), b0, 0.0)
    for a in range(3):
        for g in range(2):
            y = Y0 + ny if g else Y0 - 1
            for x in range(nx + 2):
                bpad[a, x, y:y + 1, :] = edge_out[g, a, x:x + 1, :]
    apply(bpad, 1, img.at[2])

    def u(a):
        return upad[a, 2:nx + 2, inner, :]

    def z(a):
        return apad[a, 1:nx + 1, inner, :]

    def b(a):
        return bpad[a, 1:nx + 1, inner, :]

    def dot(left, right):
        total = None
        for a in range(3):
            t = left(a) * right(a)
            total = t if total is None else total + t
        return jnp.sum(jnp.sum(total, axis=0), axis=0, keepdims=True)

    red[0:1, :] = dot(lambda a: r0[a], lambda a: own[1, a])
    red[1:2, :] = dot(u, lambda a: img[0, a])
    red[2:3, :] = dot(z, lambda a: img[0, a])
    red[3:4, :] = dot(b, lambda a: img[0, a])
    red[5:6, :] = dot(z, lambda a: img[2, a])
    red[6:7, :] = dot(b, lambda a: img[2, a])
    take(A, 0)
    apply(apad, 1, img.at[1])
    red[4:5, :] = dot(z, lambda a: img[1, a])

    rows = lax.broadcasted_iota(jnp.int32, (8, nz), 0)
    diagonal = rows == lax.broadcasted_iota(jnp.int32, (8, nz), 1)
    each = jnp.sum(red[...], axis=1, keepdims=True)
    red1[...] = jnp.sum(jnp.where(diagonal, each, 0.0), axis=0, keepdims=True)
    n = nd * nb
    me = dom * nb + bud
    rall[me] = red1[...]
    for j in sorted(range(1, n), key=lambda j: abs(2 * j - n)):
        peer = lax.rem(me + j, n)
        remote(red1, rall.at[me], ds.at[0], dr.at[0], peer // nb, lax.rem(peer, nb)).start()

    def every():
        part = rall.at[pl.ds(0, n - 1)]
        return remote(part, part, ds.at[0], dr.at[0], dom, bud)

    start_keep(2, 0)
    start_keep(2, 1)

    take(X, 0)
    apply(xpad, 1, img3)
    centre_value = (HIGH + LOW) / 2.0
    half_width = (HIGH - LOW) / 2.0
    ratio_value = centre_value / half_width
    weight = 1.0 / ratio_value
    for a in range(3):
        t = target[a] - img3[a] * stiff[...]
        d = inv[a] * t / centre_value
        target[a] = t
        update[a] = d
        solved[a] = d
        lpad[a, 1:nx + 1, inner, :] = d * stiff[...]
    for sweep in range(SWEEPS - 1):
        apply(lpad, 1, img3)
        weight_next = 1.0 / (2.0 * ratio_value - weight)
        for a in range(3):
            remain = target[a] - img3[a] * stiff[...]
            d = weight_next * weight * update[a] + (2.0 * weight_next / half_width) * (inv[a] * remain)
            y = solved[a] + d
            update[a] = d
            solved[a] = y
            if sweep < SWEEPS - 2:
                lpad[a, 1:nx + 1, inner, :] = y * stiff[...]
        weight = weight_next

    for a in range(3):
        x_out[a] = jnp.where(me_failed, solved[a], x_in[a])
    s_out[...] = stiff[...]
    for h in (U, A, X):
        end(h)
    for w in range(2):
        for i in range(3):
            for l in range(levels):
                fetch[w][i][l].wait_send()
    for w in range(3):
        for i in range(2):
            for l in range(levels):
                keep[w][i][l].wait_recv()
        for a in range(3):
            got = brecv[0, w, a]
            for l in range(1, levels):
                got = jnp.where(bit_here == l, brecv[l, w, a], got)
            other[w, a] = got

    every().wait_recv()
    total = jnp.sum(rall[...], axis=0)
    sums = jnp.sum(jnp.where(diagonal, jnp.broadcast_to(total, (8, nz)), 0.0), axis=1, keepdims=True)
    g0, c0, e0, f0, h0, h1, h2 = [jnp.broadcast_to(sums[j:j + 1], (1, nz)) for j in range(7)]
    alpha0 = g0 / c0
    g1 = g0 - 2.0 * alpha0 * e0 + alpha0 * alpha0 * f0
    beta0 = g1 / g0
    c1 = (
        h0 - 2.0 * alpha0 * h1 + alpha0 * alpha0 * h2
        + 2.0 * beta0 * (e0 - alpha0 * f0) + beta0 * beta0 * c0
    )
    alpha1 = g1 / c1
    coef[0:1, :] = alpha0
    coef[1:2, :] = beta0
    coef[2:3, :] = alpha1

    for w in range(3):
        for i in range(2):
            for l in range(levels):
                keep[w][i][l].wait_send()
    every().wait_send()


def finish(x0, r0, own, other, img, stiff, coef, x_out, r_out, b_out, xs, rs, bs, sems):
    copies = [pltpu.make_async_copy(other.at[0], b_out.at[0], sems.at[9])]
    copies[0].start()
    alpha0, beta0, alpha1 = coef[0:1, :], coef[1:2, :], coef[2:3, :]
    alpha0, beta0, alpha1 = alpha0[None], beta0[None], alpha1[None]
    for a in range(3):
        bs[a] = other[1, a] - alpha0 * other[2, a] + beta0 * other[0, a]
        p0 = own[0, a]
        p1 = own[1, a] - alpha0 * own[2, a] + beta0 * p0
        xs[a] = x0[a] + alpha0 * p0 + alpha1 * p1
        t0 = img[0, a]
        q1 = img[1, a] - alpha0 * img[2, a] + beta0 * t0
        rs[a] = r0[a] - stiff[...] * (alpha0 * t0 + alpha1 * q1)
        for i, (src, dst) in enumerate((
            (bs.at[a], b_out.at[1, a]), (xs.at[a], x_out.at[a]), (rs.at[a], r_out.at[a]),
        )):
            copies.append(pltpu.make_async_copy(src, dst, sems.at[a * 3 + i]))
            copies[-1].start()
    for c in copies:
        c.wait()


def on_device(nd, nb, rhs, stiff, coupling, x_in, r_in, p_in, backup_in, beta, fc, bb):
    levels = nb.bit_length() - 1
    nx, ny, nz = stiff.shape
    f32 = jnp.float32
    vmem = pl.BlockSpec(memory_space=pltpu.VMEM)
    smem = pl.BlockSpec(memory_space=pltpu.SMEM)
    hbm = pl.BlockSpec(memory_space=pltpu.HBM)
    field = (3, nx, ny, nz)
    dma = pltpu.SemaphoreType.DMA

    def v(*shape):
        return pltpu.VMEM(shape, f32)

    def rim(deep):
        return v(3, nx + 2 * deep, ny + 2 * Y0, nz)

    def strips(deep):
        return [v(2, 3, deep, nx, nz)] * 2 + [v(4, deep, 3, deep, nz)] * 2

    parts = pl.pallas_call(
        functools.partial(kernel, nd, nb, levels),
        out_shape=(
            v(*field), v(*field), v(3, *field), v(3, *field), v(3, *field), v(nx, ny, nz), v(8, nz),
        ),
        in_specs=[hbm] * 7 + [smem] * 3,
        out_specs=(vmem,) * 7,
        scratch_shapes=[
            v(*field), v(nx, ny, nz), pltpu.SMEM((3, 3, 27), f32), v(*field), v(*field), v(*field), v(2, *field),
            dma((7,)),
            rim(2), rim(1), rim(1), rim(1), rim(1),
            *strips(2), *strips(1), *strips(1),
            v(2, 3, 3, nx + 4, nz), v(2, 3, nx + 4, nz), v(levels, 2, *field), v(levels, 3, *field),
            v(*field), v(nx, ny, nz), v(*field), v(*field), v(*field), v(*field),
            v(8, nz), v(1, nz), v(nd * nb, 1, nz),
            *[dma((halo_sems(deep),)) for deep in (2, 1, 1) for _ in range(2)],
            dma((levels, 2, 3)), dma((levels, 2, 3)),
            dma((levels, 3, 2)), dma((levels, 3, 2)),
            dma((1,)), dma((1,)),
            pltpu.SemaphoreType.REGULAR((nd.bit_length(),)),
        ],
        compiler_params=pltpu.CompilerParams(
            collective_id=0, has_side_effects=True, vmem_limit_bytes=40 * 1024 * 1024
        ),
    )(*[pltpu.with_memory_space_constraint(v, pltpu.HBM) for v in (
        rhs, stiff, jnp.transpose(coupling, (1, 2, 0)), x_in, r_in, p_in, backup_in
    )], beta, fc, bb)
    return pl.pallas_call(
        finish,
        out_shape=(
            pltpu.HBM(field, f32), pltpu.HBM(field, f32), pltpu.HBM((2,) + field, f32),
        ),
        in_specs=[vmem] * 7,
        out_specs=(hbm, hbm, hbm),
        scratch_shapes=[
            pltpu.VMEM(field, f32), pltpu.VMEM(field, f32), pltpu.VMEM(field, f32), dma((10,)),
        ],
        compiler_params=pltpu.CompilerParams(vmem_limit_bytes=8 * 1024 * 1024),
    )(*parts)


def solution(mesh):
    nd, nb = mesh.shape["dom"], mesh.shape["bud"]
    placed = (
        P(None, "dom", "bud", None),
        P("dom", "bud", None),
        P(),
        P(None, "dom", "bud", None),
        P(None, "dom", "bud", None),
        P(None, "dom", "bud", None),
        P(None, None, "dom", "bud", None),
        P(),
        P("dom"),
        P("dom"),
    )
    return jax.shard_map(
        functools.partial(on_device, nd, nb),
        mesh=mesh,
        in_specs=placed,
        out_specs=(
            P(None, "dom", "bud", None),
            P(None, "dom", "bud", None),
            P(None, None, "dom", "bud", None),
        ),
        check_vma=False,
    )
```

time: 27.2 us -> 24.4 us (0.90)
  Pallas kernels: 24.4 us -> 21.6 us
    pallas_call x1, Pallas kernels: 23.6 us -> 20.8 us  [on_device(): pl.pallas_call(functools.partial(kernel, nd, nb, levels), out_shape=(v(*f...]
where the time goes in v2:
time: 24.4 us; the launch traced here: 24.2 us
  Pallas kernels  21.6 us (89%)
  between operations  2.58 us (11%)
    pallas_call x1, Pallas kernels, on_device(): pl.pallas_call(functools.partial(kernel, nd, nb, levels), out_shape=(v(*f...  20.8 us
    pallas_call x1, Pallas kernels, on_device(): pl.pallas_call(finish, out_shape=(pltpu.HBM(field, f32), pltpu.HBM(field,...  0.82 us

profile of v2, /device:TPU:0, one launch (start us, length us, event | category | flops | bytes accessed | tf_op | source)
XLA Modules:
  0.0 24.2 jit_solution(11262336224647948448)
XLA Ops:
  2.6 20.8 %shard_map.121 = (f32[3,4,16,128]{3,2,1,0:T(8,128)S(1)}, f32[3,4,16,128]{3,2,1,0:T(8,128)S(1)}, f32[3,3,4,16,128]{4,3,2,1,0:T(8,128)S(1)}, f32[3,3,4,16,128]{4,3...) custom-call(f32[3,4,16,128]{3,2,1,0:T(8,128)} %rhs_h.1, ...), custom_call_target="tpu_custom_call" | custom-call | tf_op jit(solution)/shard_map/pallas_call | solution.py:585
  23.3 0.8 %shard_map.122 = (f32[3,4,16,128]{3,2,1,0:T(8,128)}, f32[3,4,16,128]{3,2,1,0:T(8,128)}, f32[2,3,4,16,128]{4,3,2,1,0:T(8,128)}) custom-call(f32[3,4,16,128]{3,2,1,0:T(8,128)S(1)} %get-tuple-element.10.x0, f32[3,4,16,128]{3,2,1,0:T(8,128)S(1)} %get-tuple-element.11.r0, f32[3,3,4,16,128]{4,3,2,1,0:T(8,128)S(1)} %get-tuple-element.12.own, ...), custom_call_target="tpu_custom_call" | custom-call | tf_op jit(solution)/shard_map/pallas_call | solution.py:612

commit v3 on v2

--- a/solution.py
+++ b/solution.py
@@ -15,14 +15,14 @@
 
 
 class Halo:
-    def __init__(self, depth, pad, ysend, yrecv, csend, crecv, send, recv):
+    def __init__(self, depth, pad, ysend, yrecv, csend, crecv, recv, zero):
         self.depth, self.pad = depth, pad
         self.ysend, self.yrecv, self.csend, self.crecv = ysend, yrecv, csend, crecv
-        self.send, self.recv = send, recv
-
-
-def halo_sems(depth):
-    return 6 * depth + 2
+        self.recv, self.zero = recv, zero
+
+
+def halo_rows(nx, ny, depth):
+    return 6 * ny + 6 * depth * nx + 12 * depth
 
 
 def kernel(
@@ -35,7 +35,8 @@
     edge, edge_out, saved, brecv,
     inv, invs, img3, target, solved, update,
     red, red1, rall,
-    us, ur, as_, ar, xs, xr, ss, sr, bs, br, ds, dr, know,
+    zx, zy2, zy1, zc2, zc1, dummy,
+    hs, ur, ar, xr, ss, sr, bs, br, ds, dr, know,
 ):
     nx, ny, nz = stiff.shape
     step = 2 if nx % 2 == 0 else 1
@@ -97,92 +98,64 @@
         loads[name] = pltpu.make_async_copy(src, dst, in_sems.at[i])
         loads[name].start()
 
-    U = Halo(2, upad, yus, yur, cus, cur, us, ur)
-    A = Halo(1, apad, yas, yar, cas, car, as_, ar)
-    X = Halo(1, xpad, yxs, yxr, cxs, cxr, xs, xr)
+    for zero in (zx, zy2, zy1, zc2, zc1):
+        zero[...] = jnp.zeros(zero.shape, f32)
+    U = Halo(2, upad, yus, yur, cus, cur, ur, (zx, zy2, zc2))
+    A = Halo(1, apad, yas, yar, cas, car, ar, (zx, zy1, zc1))
+    X = Halo(1, xpad, yxs, yxr, cxs, cxr, xr, (zx, zy1, zc1))
     inner = pl.ds(Y0, ny)
 
-    for h in (U, A, X):
+    def either(sx, sy, there, beyond):
+        @pl.when(has(sx, sy))
+        def _():
+            there().start()
+
+        @pl.when(jnp.logical_not(has(sx, sy)))
+        def _():
+            beyond().start()
+
+    def send_x(h, sx, d):
         deep = h.depth
-        for sx in (-1, 1):
-            @pl.when(jnp.logical_not(has(sx, 0)))
-            def _(h=h, deep=deep, sx=sx):
-                for d in range(deep):
-                    x = deep - 1 - d if sx < 0 else deep + nx + d
-                    h.pad[:, x, inner, :] = jnp.zeros((3, ny, nz), f32)
-
-        for sy in (-1, 1):
-            @pl.when(jnp.logical_not(has(0, sy)))
-            def _(h=h, sy=sy):
-                i = 1 if sy > 0 else 0
-                h.yrecv[i] = jnp.zeros(h.yrecv.shape[1:], f32)
-
-        for q, (sx, sy) in enumerate(CORNERS):
-            @pl.when(jnp.logical_not(has(sx, sy)))
-            def _(h=h, q=q):
-                h.crecv[q] = jnp.zeros(h.crecv.shape[1:], f32)
-
-    def xface(h, sx, d):
-        deep = h.depth
+        low, high = deep - 1 - d, deep + nx + d
         src = deep + (nx - 1 - d if sx > 0 else d)
-        dst = deep - 1 - d if sx > 0 else deep + nx + d
-        i, o = (deep + d, d) if sx > 0 else (d, deep + d)
-        return remote(
-            h.pad.at[:, src, inner, :], h.pad.at[:, dst, inner, :],
-            h.send.at[i], h.recv.at[o], dom + sx, bud,
-        )
-
-    def yface(h, sy):
-        i, o = (1, 0) if sy > 0 else (0, 1)
-        return remote(
-            h.ysend.at[i], h.yrecv.at[o],
-            h.send.at[2 * h.depth + i], h.recv.at[2 * h.depth + o], dom, bud + sy,
-        )
-
-    def corner(h, q, e):
+        to, own_side = (low, high) if sx > 0 else (high, low)
+        either(sx, 0, lambda: remote(
+            h.pad.at[:, src, inner, :], h.pad.at[:, to, inner, :], hs.at[1 if sx > 0 else 0], h.recv.at[d],
+            dom + sx, bud,
+        ), lambda: pltpu.make_async_copy(h.zero[0], h.pad.at[:, own_side, inner, :], h.recv.at[d]))
+
+    def send_y(h, sy):
+        i = 1 if sy > 0 else 0
+        either(0, sy, lambda: remote(
+            h.ysend.at[i], h.yrecv.at[1 - i], hs.at[2 + i], h.recv.at[0], dom, bud + sy,
+        ), lambda: pltpu.make_async_copy(h.zero[1], h.yrecv.at[i], h.recv.at[0]))
+
+    def send_c(h, q, e):
         sx, sy = CORNERS[q]
-        base = 2 * h.depth + 2
-        return remote(
-            h.csend.at[q, e], h.crecv.at[3 - q, e],
-            h.send.at[base + q * h.depth + e], h.recv.at[base + (3 - q) * h.depth + e],
-            dom + sx, bud + sy,
-        )
-
-    def xland(h, sx, d):
-        deep = h.depth
-        x = deep + nx + d if sx > 0 else deep - 1 - d
-        i = deep + d if sx > 0 else d
-        part = h.pad.at[:, x, inner, :]
-        return remote(part, part, h.send.at[i], h.recv.at[i], dom + sx, bud)
-
-    def yland(h, sy):
-        i = 1 if sy > 0 else 0
-        part = h.yrecv.at[i]
-        return remote(part, part, h.send.at[2 * h.depth + i], h.recv.at[2 * h.depth + i], dom, bud + sy)
-
-    def cland(h, q, e):
-        sx, sy = CORNERS[q]
-        i = 2 * h.depth + 2 + q * h.depth + e
-        part = h.crecv.at[q, e]
-        return remote(part, part, h.send.at[i], h.recv.at[i], dom + sx, bud + sy)
-
-    def each_x(h, d, do):
-        for sx in (-1, 1):
-            @pl.when(has(sx, 0))
-            def _(sx=sx):
-                do(h, sx, d)
-
-    def each_y(h, do):
-        for sy in (-1, 1):
-            @pl.when(has(0, sy))
-            def _(sy=sy):
-                do(h, sy)
-
-    def each_c(h, e, do):
-        for q, (sx, sy) in enumerate(CORNERS):
+        either(sx, sy, lambda: remote(
+            h.csend.at[q, e], h.crecv.at[3 - q, e], hs.at[4 + q], h.recv.at[e], dom + sx, bud + sy,
+        ), lambda: pltpu.make_async_copy(h.zero[2], h.crecv.at[q, e], h.recv.at[e]))
+
+    def send_xc(h, sx, d):
+        for q in range(4):
+            if CORNERS[q][0] == sx:
+                pack_c(h, q, d)
+        for q in range(4):
+            if CORNERS[q][0] == sx:
+                send_c(h, q, d)
+        send_x(h, sx, d)
+
+    def end_halos():
+        deeps = (2, 1, 1)
+        for i, (sx, sy, rows) in enumerate(
+            [(sx, 0, 3 * ny * sum(deeps)) for sx in (-1, 1)]
+            + [(0, sy, 3 * nx * sum(deeps)) for sy in (-1, 1)]
+            + [(sx, sy, 3 * sum(d * d for d in deeps)) for sx, sy in CORNERS]
+        ):
             @pl.when(has(sx, sy))
-            def _(q=q):
-                do(h, q, e)
+            def _(i=i, sx=sx, sy=sy, rows=rows):
+                part = dummy.at[pl.ds(0, rows)]
+                remote(part, part, hs.at[i], hs.at[i], dom + sx, bud + sy).wait_send()
 
     def pack_y(h):
         deep = h.depth
@@ -193,14 +166,14 @@
                     for x in range(nx):
                         h.ysend[i, b, d, x:x + 1, :] = h.pad[b, deep + x, y:y + 1, :]
 
-    def pack_c(h, e):
+    def pack_c(h, q, e):
         deep = h.depth
-        for q, (sx, sy) in enumerate(CORNERS):
-            x = deep + (nx - 1 - e if sx > 0 else e)
-            for b in range(3):
-                for d in range(deep):
-                    y = Y0 + (ny - deep + d if sy > 0 else d)
-                    h.csend[q, e, b, d:d + 1, :] = h.pad[b, x, y:y + 1, :]
+        sx, sy = CORNERS[q]
+        x = deep + (nx - 1 - e if sx > 0 else e)
+        for b in range(3):
+            for d in range(deep):
+                y = Y0 + (ny - deep + d if sy > 0 else d)
+                h.csend[q, e, b, d:d + 1, :] = h.pad[b, x, y:y + 1, :]
 
     def unpack_y(h):
         deep = h.depth
@@ -218,28 +191,13 @@
             for b in range(3):
                 h.pad[b, x, y:y + 1, :] = h.crecv[q, e, b, d:d + 1, :]
 
-    def start_x(h, d):
-        each_x(h, d, lambda *a: xface(*a).start())
-
-    def start_y(h):
-        each_y(h, lambda *a: yface(*a).start())
-
-    def start_c(h, e):
-        each_c(h, e, lambda *a: corner(*a).start())
-
     def take(h, d):
-        each_x(h, d, lambda *a: xland(*a).wait_recv())
-        each_c(h, d, lambda *a: cland(*a).wait_recv())
+        rows = 6 * ny + 12 * h.depth + (6 * h.depth * nx if d == 0 else 0)
+        part = dummy.at[pl.ds(0, rows)]
+        pltpu.make_async_copy(part, part, h.recv.at[d]).wait()
         if d == 0:
-            each_y(h, lambda *a: yland(*a).wait_recv())
             unpack_y(h)
         unpack_c(h, d)
-
-    def end(h):
-        for d in range(h.depth):
-            each_x(h, d, lambda *a: xface(*a).wait_send())
-            each_c(h, d, lambda *a: corner(*a).wait_send())
-        each_y(h, lambda *a: yface(*a).wait_send())
 
     def stencil(load, groups):
         acc = [[[None] * groups for _ in range(3)] for _ in range(3)]
@@ -282,20 +240,28 @@
     for a in range(3):
         xpad[a, 1:nx + 1, inner, :] = jnp.where(me_failed, 0.0, x_in[a] * stiff[...])
     pack_y(X)
-    pack_c(X, 0)
 
     pl.semaphore_wait(barrier, nb - 1 + ahead(1))
 
-    pieces = [pl.ds(0, 1), pl.ds(nx - 1, 1), pl.ds(1, nx - 2)]
-    fetch = [[[remote(bk.at[w, :, x], saved.at[l, w, :, x], ss.at[l, w, i], sr.at[l, w, i], dom, flip(l))
-               for l in range(levels)] for i, x in enumerate(pieces)] for w in range(2)]
+    order = [slice(x, x + 1) for x in (0, nx - 1, 1, nx - 2)] + ([slice(2, nx - 2)] if nx > 4 else [])
     for w in (1, 0):
-        for i in range(3):
+        for i, x in enumerate(order):
+            x = pl.ds(x.start, x.stop - x.start)
             for l in range(levels):
-                fetch[w][i][l].start()
+                remote(
+                    bk.at[w, :, x], saved.at[l, w, :, x], ss.at[0], sr.at[w, i], dom, flip(l)
+                ).start()
+
+    def fetched(w, i):
+        x = order[i]
+        part = saved.at[:, w, :, pl.ds(x.start, x.stop - x.start)]
+        pltpu.make_async_copy(part, part, sr.at[w, i]).wait()
+
     greet_near(know.at[0])
-    start_x(X, 0)
-    start_y(X)
+    for sx in (-1, 1):
+        send_x(X, sx, 0)
+    for sy in (-1, 1):
+        send_y(X, sy)
 
     coef[...] = jnp.zeros(coef.shape, f32)
     red[...] = jnp.zeros(red.shape, f32)
@@ -311,7 +277,10 @@
     pl.semaphore_wait(know.at[0], nb - 1 + ahead(1))
     if len(strides) > 1:
         greet_dom(know.at[1], strides[1])
-    start_c(X, 0)
+    for q in range(4):
+        pack_c(X, q, 0)
+    for q in range(4):
+        send_c(X, q, 0)
 
     def pick(value, l_of):
         got = l_of(0)
@@ -326,32 +295,20 @@
             upad[a, x.start + 2:x.stop + 2, inner, :] = p0 * stiff[x]
 
     loads["p"].wait()
-    for i in (0, 1):
+    for i, x in enumerate(order):
+        fetched(1, i)
+        start_field(x)
+        if i < 4:
+            send_xc(U, (-1, 1)[i % 2], i // 2)
+    pack_y(U)
+    for sy in (-1, 1):
+        send_y(U, sy)
+
+    def start_keep(w, x):
         for l in range(levels):
-            fetch[1][i][l].wait_recv()
-    start_field(slice(0, 1))
-    start_field(slice(nx - 1, nx))
-    pack_c(U, 0)
-    start_c(U, 0)
-    start_x(U, 0)
-    for l in range(levels):
-        fetch[1][2][l].wait_recv()
-    start_field(slice(1, nx - 1))
-    pack_c(U, 1)
-    start_c(U, 1)
-    start_x(U, 1)
-    pack_y(U)
-    start_y(U)
-
-    keep = [[[remote(own.at[w, :, x], brecv.at[l, w, :, x], bs.at[l, w, i], br.at[l, w, i], dom, flip(l))
-              for l in range(levels)] for i, x in enumerate((pl.ds(0, nx // 2), pl.ds(nx // 2, nx - nx // 2)))]
-            for w in range(3)]
-
-    def start_keep(w, i):
-        for l in range(levels):
-            keep[w][i][l].start()
-
-    start_keep(0, 0)
+            remote(own.at[w, :, x], brecv.at[l, w, :, x], bs.at[0], br.at[0], dom, flip(l)).start()
+
+    start_keep(0, pl.ds(0, nx - 1))
     for i in range(1, len(strides)):
         pl.semaphore_wait(know.at[i], ahead(strides[i]))
         if i + 1 < len(strides):
@@ -370,22 +327,16 @@
 
     for name in ("r", "rhs"):
         loads[name].wait()
-    for i in (0, 1):
-        for l in range(levels):
-            fetch[0][i][l].wait_recv()
-    second_field(slice(0, 1))
-    second_field(slice(nx - 1, nx))
-    pack_c(A, 0)
-    start_c(A, 0)
-    start_x(A, 0)
-    for l in range(levels):
-        fetch[0][2][l].wait_recv()
-    second_field(slice(1, nx - 1))
+    for i, x in enumerate(order):
+        fetched(0, i)
+        second_field(x)
+        if i < 2:
+            send_xc(A, (-1, 1)[i], 0)
     pack_y(A)
-    start_y(A)
-    start_keep(0, 1)
-    start_keep(1, 0)
-    start_keep(1, 1)
+    for sy in (-1, 1):
+        send_y(A, sy)
+    start_keep(0, pl.ds(nx - 1, 1))
+    start_keep(1, pl.ds(0, nx))
 
     take(U, 0)
     apply(upad, 2, img.at[0])
@@ -462,16 +413,18 @@
     n = nd * nb
     me = dom * nb + bud
     rall[me] = red1[...]
-    for j in sorted(range(1, n), key=lambda j: abs(2 * j - n)):
-        peer = lax.rem(me + j, n)
-        remote(red1, rall.at[me], ds.at[0], dr.at[0], peer // nb, lax.rem(peer, nb)).start()
+    bits = [(1 << i) * (1 - 2 * lax.rem(dom // (1 << i), 2)) for i in range((nd - 1).bit_length())]
+    for mask in range(nd - 1, -1, -1):
+        to = dom + sum(bit for i, bit in enumerate(bits) if mask >> i & 1)
+        for j in range(nb):
+            if mask or j:
+                remote(red1, rall.at[me], ds.at[0], dr.at[0], to, lax.rem(bud + j, nb)).start()
 
     def every():
         part = rall.at[pl.ds(0, n - 1)]
         return remote(part, part, ds.at[0], dr.at[0], dom, bud)
 
-    start_keep(2, 0)
-    start_keep(2, 1)
+    start_keep(2, pl.ds(0, nx))
 
     take(X, 0)
     apply(xpad, 1, img3)
@@ -502,16 +455,16 @@
     for a in range(3):
         x_out[a] = jnp.where(me_failed, solved[a], x_in[a])
     s_out[...] = stiff[...]
-    for h in (U, A, X):
-        end(h)
-    for w in range(2):
-        for i in range(3):
-            for l in range(levels):
-                fetch[w][i][l].wait_send()
+    end_halos()
+
+    def all_of(ref, sem):
+        return remote(ref, ref, sem.at[0], sem.at[0], dom, bud)
+
+    all_of(saved, ss).wait_send()
+    all_of(brecv, bs).wait_send()
+    every().wait_send()
+    pltpu.make_async_copy(brecv, brecv, br.at[0]).wait()
     for w in range(3):
-        for i in range(2):
-            for l in range(levels):
-                keep[w][i][l].wait_recv()
         for a in range(3):
             got = brecv[0, w, a]
             for l in range(1, levels):
@@ -534,12 +487,6 @@
     coef[1:2, :] = beta0
     coef[2:3, :] = alpha1
 
-    for w in range(3):
-        for i in range(2):
-            for l in range(levels):
-                keep[w][i][l].wait_send()
-    every().wait_send()
-
 
 def finish(x0, r0, own, other, img, stiff, coef, x_out, r_out, b_out, xs, rs, bs, sems):
     copies = [pltpu.make_async_copy(other.at[0], b_out.at[0], sems.at[9])]
@@ -597,11 +544,12 @@
             v(2, 3, 3, nx + 4, nz), v(2, 3, nx + 4, nz), v(levels, 2, *field), v(levels, 3, *field),
             v(*field), v(nx, ny, nz), v(*field), v(*field), v(*field), v(*field),
             v(8, nz), v(1, nz), v(nd * nb, 1, nz),
-            *[dma((halo_sems(deep),)) for deep in (2, 1, 1) for _ in range(2)],
-            dma((levels, 2, 3)), dma((levels, 2, 3)),
-            dma((levels, 3, 2)), dma((levels, 3, 2)),
-            dma((1,)), dma((1,)),
-            pltpu.SemaphoreType.REGULAR((nd.bit_length(),)),
+            v(3, ny, nz), v(3, 2, nx, nz), v(3, 1, nx, nz), v(3, 2, nz), v(3, 1, nz),
+            v(max(12 * ny, halo_rows(nx, ny, 2)), 1, nz),
+            dma((8,)), dma((2,)), dma((1,)), dma((1,)),
+            dma((1,)), dma((2, 4 if nx == 4 else 5)),
+            dma((1,)), dma((1,)), dma((1,)), dma((1,)),
+            pltpu.SemaphoreType.REGULAR((max((nd - 1).bit_length(), 1),)),
         ],
         compiler_params=pltpu.CompilerParams(
             collective_id=0, has_side_effects=True, vmem_limit_bytes=40 * 1024 * 1024

time: 24.4 us -> 23.3 us (0.955)
  Pallas kernels: 21.6 us -> 20.5 us
    pallas_call x1, Pallas kernels: 20.8 us -> 19.7 us  [on_device(): pl.pallas_call(functools.partial(kernel, nd, nb, levels), out_shape=(v(*f...]
where the time goes in v3:
time: 23.3 us; the launch traced here: 23.1 us
  Pallas kernels  20.5 us (88%)
  between operations  2.58 us (11%)
    pallas_call x1, Pallas kernels, on_device(): pl.pallas_call(functools.partial(kernel, nd, nb, levels), out_shape=(v(*f...  19.7 us
    pallas_call x1, Pallas kernels, on_device(): pl.pallas_call(finish, out_shape=(pltpu.HBM(field, f32), pltpu.HBM(field,...  0.82 us

profile of v3, /device:TPU:0, one launch (start us, length us, event | category | flops | bytes accessed | tf_op | source)
XLA Modules:
  0.0 23.1 jit_solution(12711430835922960583)
XLA Ops:
  2.6 19.7 %shard_map.121 = (f32[3,4,16,128]{3,2,1,0:T(8,128)S(1)}, f32[3,4,16,128]{3,2,1,0:T(8,128)S(1)}, f32[3,3,4,16,128]{4,3,2,1,0:T(8,128)S(1)}, f32[3,3,4,16,128]{4,3...) custom-call(f32[3,4,16,128]{3,2,1,0:T(8,128)} %rhs_h.1, ...), custom_call_target="tpu_custom_call" | custom-call | tf_op jit(solution)/shard_map/pallas_call | solution.py:532
  22.3 0.8 %shard_map.122 = (f32[3,4,16,128]{3,2,1,0:T(8,128)}, f32[3,4,16,128]{3,2,1,0:T(8,128)}, f32[2,3,4,16,128]{4,3,2,1,0:T(8,128)}) custom-call(f32[3,4,16,128]{3,2,1,0:T(8,128)S(1)} %get-tuple-element.10.x0, f32[3,4,16,128]{3,2,1,0:T(8,128)S(1)} %get-tuple-element.11.r0, f32[3,3,4,16,128]{4,3,2,1,0:T(8,128)S(1)} %get-tuple-element.12.own, ...), custom_call_target="tpu_custom_call" | custom-call | tf_op jit(solution)/shard_map/pallas_call | solution.py:560

commit v4 on v3

--- a/solution.py
+++ b/solution.py
@@ -32,7 +32,7 @@
     rhs, stiff, cpl, x_in, r_in, p_in, bk, in_sems,
     upad, apad, xpad, bpad, lpad,
     yus, yur, cus, cur, yas, yar, cas, car, yxs, yxr, cxs, cxr,
-    edge, edge_out, saved, brecv,
+    edge, urim, arim, brim, ytmp, saved, brecv,
     inv, invs, img3, target, solved, update,
     red, red1, rall,
     zx, zy2, zy1, zc2, zc1, dummy,
@@ -175,12 +175,12 @@
                 y = Y0 + (ny - deep + d if sy > 0 else d)
                 h.csend[q, e, b, d:d + 1, :] = h.pad[b, x, y:y + 1, :]
 
-    def unpack_y(h):
+    def unpack_y(h, xs):
         deep = h.depth
         for i in range(2):
             y, d = (Y0 + ny, 0) if i else (Y0 - 1, deep - 1)
             for b in range(3):
-                for x in range(nx):
+                for x in xs:
                     h.pad[b, deep + x, y:y + 1, :] = h.yrecv[i, b, d, x:x + 1, :]
 
     def unpack_c(h, e):
@@ -195,8 +195,6 @@
         rows = 6 * ny + 12 * h.depth + (6 * h.depth * nx if d == 0 else 0)
         part = dummy.at[pl.ds(0, rows)]
         pltpu.make_async_copy(part, part, h.recv.at[d]).wait()
-        if d == 0:
-            unpack_y(h)
         unpack_c(h, d)
 
     def stencil(load, groups):
@@ -205,10 +203,14 @@
             for dy in range(3):
                 for b in range(3):
                     ws = [load(b, dx, dy, g) for g in range(groups)]
+                    if all(w is None for w in ws):
+                        continue
                     for dz in range(3):
                         o = (dx * 3 + dy) * 3 + dz
                         for a in range(3):
                             for g in range(groups):
+                                if ws[g] is None:
+                                    continue
                                 term = cpl[a, b, o] * ws[g]
                                 old = acc[dz][a][g]
                                 acc[dz][a][g] = term if old is None else old + term
@@ -232,6 +234,49 @@
                 for g in range(step):
                     out[a, x + g] = got[a][g]
 
+    def from_own(pad, deep, out):
+        for x in range(0, nx, step):
+            got = stencil(
+                lambda b, dx, dy, g: pad[b, x + g + deep - 1 + dx, Y0 - 1 + dy:Y0 - 1 + dy + ny, :]
+                if 0 <= x + g + dx - 1 < nx else None, step
+            )
+            for a in range(3):
+                for g in range(step):
+                    out[a, x + g] = got[a][g]
+
+    def from_row(pad, deep, out, source, touched):
+        targets = [x for x in (source - 1, source, source + 1) if 0 <= x < nx]
+        for xs in (targets[:2], targets[2:]):
+            if not xs:
+                continue
+            got = stencil(
+                lambda b, dx, dy, g: pad[b, source + deep, Y0 - 1 + dy:Y0 - 1 + dy + ny, :]
+                if dx == source - xs[g] + 1 else None, len(xs)
+            )
+            for a in range(3):
+                for g, x in enumerate(xs):
+                    out[a, x] = out[a, x] + got[a][g] if x in touched else got[a][g]
+            touched.update(xs)
+
+    def from_rim(pad, deep, strip, out):
+        got = stencil(
+            lambda b, dx, dy, g: strip[g, b, dx:dx + nx, :] if dy == 2 * g else None, 2
+        )
+        for a in range(3):
+            for g in range(2):
+                ytmp[g, a, 0:nx, :] = got[a][g]
+        got = stencil(
+            lambda b, dx, dy, g: pad[b, deep + nx if g else deep - 1, Y0 - 1 + dy:Y0 - 1 + dy + ny, :]
+            if dx == 2 * g else None, 2
+        )
+        for a in range(3):
+            for g, x in enumerate((0, nx - 1)):
+                out[a, x] = out[a, x] + got[a][g]
+        for a in range(3):
+            for g, y in enumerate((0, ny - 1)):
+                for x in range(nx):
+                    out[a, x, y:y + 1, :] = out[a, x, y:y + 1, :] + ytmp[g, a, x:x + 1, :]
+
     for name in ("cpl", "stiff", "x", "bk"):
         loads[name].wait()
     me_failed = jnp.full((1, ny, nz), fc[0], jnp.int32) == bud
@@ -269,6 +314,12 @@
         lpad[:, x] = jnp.zeros((3, ny + 2 * Y0, nz), f32)
     for y in (0, Y0 + ny):
         lpad[:, 1:nx + 1, y:y + Y0, :] = jnp.zeros((3, nx, Y0, nz), f32)
+    for pad, deep in ((upad, 2), (apad, 1), (bpad, 1)):
+        for y in (0, Y0 + ny):
+            pad[:, deep:nx + deep, y:y + Y0, :] = jnp.zeros((3, nx, Y0, nz), f32)
+    for strip in (urim, arim, brim):
+        for x in (0, nx + 1):
+            strip[:, :, x:x + 1, :] = jnp.zeros((2, 3, 1, nz), f32)
     invs[...] = 1.0 / stiff[...]
     inv_centre = [1.0 / jnp.full((1, nz), centre[a], f32) for a in range(3)]
     for a in range(3):
@@ -309,10 +360,12 @@
             remote(own.at[w, :, x], brecv.at[l, w, :, x], bs.at[0], br.at[0], dom, flip(l)).start()
 
     start_keep(0, pl.ds(0, nx - 1))
-    for i in range(1, len(strides)):
+    from_own(upad, 2, img.at[0])
+    def know_step(i):
         pl.semaphore_wait(know.at[i], ahead(strides[i]))
         if i + 1 < len(strides):
             greet_dom(know.at[i + 1], strides[i + 1])
+
 
     def second_field(x):
         for a in range(3):
@@ -327,37 +380,80 @@
 
     for name in ("r", "rhs"):
         loads[name].wait()
+    touched = set()
     for i, x in enumerate(order):
         fetched(0, i)
         second_field(x)
+        if i == 1 and len(strides) > 1:
+            know_step(1)
         if i < 2:
             send_xc(A, (-1, 1)[i], 0)
-    pack_y(A)
-    for sy in (-1, 1):
-        send_y(A, sy)
-    start_keep(0, pl.ds(nx - 1, 1))
-    start_keep(1, pl.ds(0, nx))
+        if i == len(order) - 1:
+            pack_y(A)
+            for sy in (-1, 1):
+                send_y(A, sy)
+            start_keep(0, pl.ds(nx - 1, 1))
+            start_keep(1, pl.ds(0, nx))
+        for source in range(x.start, x.stop):
+            from_row(apad, 1, img.at[1], source, touched)
+
+    def strip_of(h, strip):
+        for i in range(2):
+            for b in range(3):
+                strip[i, b, 1:nx + 1, :] = h.yrecv[i, b, 0 if i else h.depth - 1]
 
     take(U, 0)
-    apply(upad, 2, img.at[0])
+    strip_of(U, urim)
+    from_rim(upad, 2, urim, img.at[0])
     for a in range(3):
         b0 = img[0, a] * inv_centre[a]
         bpad[a, 1:nx + 1, inner, :] = b0
         own[2, a] = b0 * invs[...]
-    take(U, 1)
+    from_own(bpad, 1, img.at[2])
+
+    def of_u(a):
+        return upad[a, 2:nx + 2, inner, :]
+
+    def of_z(a):
+        return apad[a, 1:nx + 1, inner, :]
+
+    def of_b(a):
+        return bpad[a, 1:nx + 1, inner, :]
+
+    def dot(left, right):
+        total = None
+        for a in range(3):
+            t = left(a) * right(a)
+            total = t if total is None else total + t
+        return jnp.sum(jnp.sum(total, axis=0), axis=0, keepdims=True)
+
+    red[0:1, :] = dot(lambda a: r0[a], lambda a: own[1, a])
+    red[1:2, :] = dot(of_u, lambda a: img[0, a])
+    red[2:3, :] = dot(of_z, lambda a: img[0, a])
+    red[3:4, :] = dot(of_b, lambda a: img[0, a])
+    unpack_y(U, (0, nx - 1))
+    def edges(layers):
+        for b in range(3):
+            for i in range(2):
+                y = Y0 + (ny - 1 if i else 0)
+                for q, (sx, sy) in enumerate(CORNERS):
+                    if (sy > 0) == bool(i):
+                        for e in layers:
+                            x = nx + 2 + e if sx > 0 else 1 - e
+                            edge[i, b, 0 if i else 2, x:x + 1, :] = upad[b, x, y:y + 1, :]
+                            for d in range(2):
+                                edge[i, b, i + d, x:x + 1, :] = cur[q, e, b, d:d + 1, :]
+
     for b in range(3):
         for i in range(2):
             for d in range(2):
-                lev = i + d
-                edge[i, b, lev, 2:nx + 2, :] = yur[i, b, d]
-                for q, (sx, sy) in enumerate(CORNERS):
-                    if (sy > 0) == bool(i):
-                        for e in range(2):
-                            x = nx + 2 + e if sx > 0 else 1 - e
-                            edge[i, b, lev, x:x + 1, :] = cur[q, e, b, d:d + 1, :]
+                edge[i, b, i + d, 2:nx + 2, :] = yur[i, b, d]
             y = Y0 + (ny - 1 if i else 0)
-            for x in range(nx + 4):
+            for x in range(2, nx + 2):
                 edge[i, b, 0 if i else 2, x:x + 1, :] = upad[b, x, y:y + 1, :]
+    edges((0,))
+    take(U, 1)
+    edges((1,))
 
     rim = stencil(lambda b, dx, dy, g: upad[b, (nx + 1 if g else 0) + dx, Y0 - 1 + dy:Y0 - 1 + dy + ny, :], 2)
     for a in range(3):
@@ -372,44 +468,29 @@
     for a in range(3):
         for g, sy in enumerate((-1, 1)):
             b0 = jnp.where(inside, rim[a][g] * inv_centre[a], 0.0)
-            edge_out[g, a, 0:nx + 2, :] = jnp.where(has(0, sy), b0, 0.0)
+            b0 = jnp.where(has(0, sy), b0, 0.0)
+            ytmp[g, a] = b0
+            brim[g, a, 1:nx + 1, :] = b0[1:nx + 1]
     for a in range(3):
         for g in range(2):
             y = Y0 + ny if g else Y0 - 1
-            for x in range(nx + 2):
-                bpad[a, x, y:y + 1, :] = edge_out[g, a, x:x + 1, :]
-    apply(bpad, 1, img.at[2])
-
-    def u(a):
-        return upad[a, 2:nx + 2, inner, :]
-
-    def z(a):
-        return apad[a, 1:nx + 1, inner, :]
-
-    def b(a):
-        return bpad[a, 1:nx + 1, inner, :]
-
-    def dot(left, right):
-        total = None
-        for a in range(3):
-            t = left(a) * right(a)
-            total = t if total is None else total + t
-        return jnp.sum(jnp.sum(total, axis=0), axis=0, keepdims=True)
-
-    red[0:1, :] = dot(lambda a: r0[a], lambda a: own[1, a])
-    red[1:2, :] = dot(u, lambda a: img[0, a])
-    red[2:3, :] = dot(z, lambda a: img[0, a])
-    red[3:4, :] = dot(b, lambda a: img[0, a])
-    red[5:6, :] = dot(z, lambda a: img[2, a])
-    red[6:7, :] = dot(b, lambda a: img[2, a])
+            for x in (0, nx + 1):
+                bpad[a, x, y:y + 1, :] = ytmp[g, a, x:x + 1, :]
+    from_rim(bpad, 1, brim, img.at[2])
+
+    red[5:6, :] = dot(of_z, lambda a: img[2, a])
+    red[6:7, :] = dot(of_b, lambda a: img[2, a])
     take(A, 0)
-    apply(apad, 1, img.at[1])
-    red[4:5, :] = dot(z, lambda a: img[1, a])
+    strip_of(A, arim)
+    from_rim(apad, 1, arim, img.at[1])
+    red[4:5, :] = dot(of_z, lambda a: img[1, a])
 
     rows = lax.broadcasted_iota(jnp.int32, (8, nz), 0)
     diagonal = rows == lax.broadcasted_iota(jnp.int32, (8, nz), 1)
     each = jnp.sum(red[...], axis=1, keepdims=True)
     red1[...] = jnp.sum(jnp.where(diagonal, each, 0.0), axis=0, keepdims=True)
+    for i in range(2, len(strides)):
+        know_step(i)
     n = nd * nb
     me = dom * nb + bud
     rall[me] = red1[...]
@@ -427,6 +508,7 @@
     start_keep(2, pl.ds(0, nx))
 
     take(X, 0)
+    unpack_y(X, range(nx))
     apply(xpad, 1, img3)
     centre_value = (HIGH + LOW) / 2.0
     half_width = (HIGH - LOW) / 2.0
@@ -541,7 +623,7 @@
             dma((7,)),
             rim(2), rim(1), rim(1), rim(1), rim(1),
             *strips(2), *strips(1), *strips(1),
-            v(2, 3, 3, nx + 4, nz), v(2, 3, nx + 4, nz), v(levels, 2, *field), v(levels, 3, *field),
+            v(2, 3, 3, nx + 4, nz), *[v(2, 3, nx + 2, nz)] * 3, v(2, 3, nx + 2, nz), v(levels, 2, *field), v(levels, 3, *field),
             v(*field), v(nx, ny, nz), v(*field), v(*field), v(*field), v(*field),
             v(8, nz), v(1, nz), v(nd * nb, 1, nz),
             v(3, ny, nz), v(3, 2, nx, nz), v(3, 1, nx, nz), v(3, 2, nz), v(3, 1, nz),

time: 23.3 us -> 22.9 us (0.983)
  Pallas kernels: 20.5 us -> 20.1 us
    pallas_call x1, Pallas kernels: 19.7 us -> 19.3 us  [on_device(): pl.pallas_call(functools.partial(kernel, nd, nb, levels), out_shape=(v(*f...]
where the time goes in v4:
time: 22.9 us; the launch traced here: 22.7 us
  Pallas kernels  20.1 us (88%)
  between operations  2.58 us (11%)
    pallas_call x1, Pallas kernels, on_device(): pl.pallas_call(functools.partial(kernel, nd, nb, levels), out_shape=(v(*f...  19.3 us
    pallas_call x1, Pallas kernels, on_device(): pl.pallas_call(finish, out_shape=(pltpu.HBM(field, f32), pltpu.HBM(field,...  0.82 us

profile of v4, /device:TPU:0, one launch (start us, length us, event | category | flops | bytes accessed | tf_op | source)
XLA Modules:
  0.0 22.7 jit_solution(11474563638565608150)
XLA Ops:
  2.6 19.3 %shard_map.121 = (f32[3,4,16,128]{3,2,1,0:T(8,128)S(1)}, f32[3,4,16,128]{3,2,1,0:T(8,128)S(1)}, f32[3,3,4,16,128]{4,3,2,1,0:T(8,128)S(1)}, f32[3,3,4,16,128]{4,3...) custom-call(f32[3,4,16,128]{3,2,1,0:T(8,128)} %rhs_h.1, ...), custom_call_target="tpu_custom_call" | custom-call | tf_op jit(solution)/shard_map/pallas_call | solution.py:614
  21.8 0.8 %shard_map.122 = (f32[3,4,16,128]{3,2,1,0:T(8,128)}, f32[3,4,16,128]{3,2,1,0:T(8,128)}, f32[2,3,4,16,128]{4,3,2,1,0:T(8,128)}) custom-call(f32[3,4,16,128]{3,2,1,0:T(8,128)S(1)} %get-tuple-element.10.x0, f32[3,4,16,128]{3,2,1,0:T(8,128)S(1)} %get-tuple-element.11.r0, f32[3,3,4,16,128]{4,3,2,1,0:T(8,128)S(1)} %get-tuple-element.12.own, ...), custom_call_target="tpu_custom_call" | custom-call | tf_op jit(solution)/shard_map/pallas_call | solution.py:642

commit v5 on v4

--- a/solution.py
+++ b/solution.py
@@ -83,16 +83,16 @@
             greet(sem, dom + stride, bud)
 
     def greet_near(sem):
-        greet_dom(sem, 1)
         for j in range(1, nb):
             greet(sem, dom, lax.rem(bud + j, nb))
+        greet_dom(sem, 1)
 
     strides = [1 << i for i in range(max(nd - 1, 1).bit_length())]
     greet_near(barrier)
 
     loads = {}
     for i, (name, src, dst) in enumerate((
-        ("cpl", cpl_h, cpl), ("bk", bk_h, bk), ("stiff", stiff_h, stiff), ("x", x_h, x_in),
+        ("bk", bk_h, bk), ("cpl", cpl_h, cpl), ("stiff", stiff_h, stiff), ("x", x_h, x_in),
         ("p", p_h, p_in), ("r", r_h, r_in), ("rhs", rhs_h, rhs),
     )):
         loads[name] = pltpu.make_async_copy(src, dst, in_sems.at[i])
@@ -277,15 +277,7 @@
                 for x in range(nx):
                     out[a, x, y:y + 1, :] = out[a, x, y:y + 1, :] + ytmp[g, a, x:x + 1, :]
 
-    for name in ("cpl", "stiff", "x", "bk"):
-        loads[name].wait()
-    me_failed = jnp.full((1, ny, nz), fc[0], jnp.int32) == bud
-    bit_here = jnp.full((1, ny, nz), bb[0], jnp.int32)
-    centre = [cpl[a, a, 13] for a in range(3)]
-    for a in range(3):
-        xpad[a, 1:nx + 1, inner, :] = jnp.where(me_failed, 0.0, x_in[a] * stiff[...])
-    pack_y(X)
-
+    loads["bk"].wait()
     pl.semaphore_wait(barrier, nb - 1 + ahead(1))
 
     order = [slice(x, x + 1) for x in (0, nx - 1, 1, nx - 2)] + ([slice(2, nx - 2)] if nx > 4 else [])
@@ -303,6 +295,15 @@
         pltpu.make_async_copy(part, part, sr.at[w, i]).wait()
 
     greet_near(know.at[0])
+    for name in ("cpl", "stiff", "x"):
+        loads[name].wait()
+    me_failed = jnp.full((1, ny, nz), fc[0], jnp.int32) == bud
+    bit_here = jnp.full((1, ny, nz), bb[0], jnp.int32)
+    centre = [cpl[a, a, 13] for a in range(3)]
+    for a in range(3):
+        xpad[a, 1:nx + 1, inner, :] = jnp.where(me_failed, 0.0, x_in[a] * stiff[...])
+    pack_y(X)
+
     for sx in (-1, 1):
         send_x(X, sx, 0)
     for sy in (-1, 1):
@@ -393,7 +394,7 @@
             for sy in (-1, 1):
                 send_y(A, sy)
             start_keep(0, pl.ds(nx - 1, 1))
-            start_keep(1, pl.ds(0, nx))
+            start_keep(1, pl.ds(0, nx - 1))
         for source in range(x.start, x.stop):
             from_row(apad, 1, img.at[1], source, touched)
 
@@ -408,7 +409,6 @@
     for a in range(3):
         b0 = img[0, a] * inv_centre[a]
         bpad[a, 1:nx + 1, inner, :] = b0
-        own[2, a] = b0 * invs[...]
     from_own(bpad, 1, img.at[2])
 
     def of_u(a):
@@ -505,6 +505,9 @@
         part = rall.at[pl.ds(0, n - 1)]
         return remote(part, part, ds.at[0], dr.at[0], dom, bud)
 
+    start_keep(1, pl.ds(nx - 1, 1))
+    for a in range(3):
+        own[2, a] = of_b(a) * invs[...]
     start_keep(2, pl.ds(0, nx))
 
     take(X, 0)

time: 22.9 us -> 22.8 us (level)
  no operation moved by 1% of the time
where the time goes in v5:
time: 22.8 us; the launch traced here: 22.6 us
  Pallas kernels  20.1 us (88%)
  between operations  2.58 us (11%)
    pallas_call x1, Pallas kernels, on_device(): pl.pallas_call(functools.partial(kernel, nd, nb, levels), out_shape=(v(*f...  19.2 us
    pallas_call x1, Pallas kernels, on_device(): pl.pallas_call(finish, out_shape=(pltpu.HBM(field, f32), pltpu.HBM(field,...  0.82 us

profile of v5, /device:TPU:0, one launch (start us, length us, event | category | flops | bytes accessed | tf_op | source)
XLA Modules:
  0.0 22.6 jit_solution(5512102915325616472)
XLA Ops:
  2.6 19.2 %shard_map.121 = (f32[3,4,16,128]{3,2,1,0:T(8,128)S(1)}, f32[3,4,16,128]{3,2,1,0:T(8,128)S(1)}, f32[3,3,4,16,128]{4,3,2,1,0:T(8,128)S(1)}, f32[3,3,4,16,128]{4,3...) custom-call(f32[3,4,16,128]{3,2,1,0:T(8,128)} %rhs_h.1, ...), custom_call_target="tpu_custom_call" | custom-call | tf_op jit(solution)/shard_map/pallas_call | solution.py:617
  21.8 0.8 %shard_map.122 = (f32[3,4,16,128]{3,2,1,0:T(8,128)}, f32[3,4,16,128]{3,2,1,0:T(8,128)}, f32[2,3,4,16,128]{4,3,2,1,0:T(8,128)}) custom-call(f32[3,4,16,128]{3,2,1,0:T(8,128)S(1)} %get-tuple-element.10.x0, f32[3,4,16,128]{3,2,1,0:T(8,128)S(1)} %get-tuple-element.11.r0, f32[3,3,4,16,128]{4,3,2,1,0:T(8,128)S(1)} %get-tuple-element.12.own, ...), custom_call_target="tpu_custom_call" | custom-call | tf_op jit(solution)/shard_map/pallas_call | solution.py:645
